TPU v7x, 256 devices: a whole 4x4x8 slice. The times are simulated.
256 devices in a mesh: seq: 64 (over y, z, core), head: 4 (over x).
Axes of the slice: x: 4, y: 4, z: 8, core: 2. Of those that a mesh axis runs over, the one named last changes fastest.
Arguments:
- tokens: bfloat16 [16384, 2048], P('seq')
- w_qkv: bfloat16 [2048, 3, 2048], P(None, None, 'head'), may hold values from -0.125 to 0.125
- w_out: bfloat16 [2048, 2048], P('head'), may hold values from -0.125 to 0.125
- norm_gain: float32 [2048], replicated, may hold values from 0.25 to 1.75
- w_label: bfloat16 [2048, 128], replicated, may hold values from -0.125 to 0.125
- offset_mid: int32 [16], P('head'), may hold values from 0 to 7
- offset_far: int32 [16], P('head'), may hold values from 0 to 63
Outputs:
- logits: float32 [16384, 128], P('seq')
All inputs are finite; a program needn't handle non-finite values.
Results may differ from a plain program's by a relative error of at most 0.023.
The roundings to bfloat16 on the way count: a program that leaves them out, or rounds other values in their place, can miss the bound.
Values may be sent and summed in bfloat16 or wider, within the bound.
No kernel may reach another device: no remote copies, remote signals or barrier semaphores. Data moves between devices by JAX's collectives and lax.ppermute only.
A program may use at most 64 MiB of HBM per device.

v0:
```python
import jax
import jax.numpy as jnp
from jax import lax
from jax.sharding import PartitionSpec as P

SPAN = 8


def from_behind(block, axis, distance):
    devices = range(lax.axis_size(axis))
    route = [((i - distance) % len(devices), i) for i in devices]
    return lax.ppermute(block, axis, route)


def attend(queries, keys, values):
    scores = jnp.einsum(
        "rhe,she->hrs", queries, keys, preferred_element_type=jnp.float32
    ) / jnp.sqrt(jnp.float32(queries.shape[2]))
    top = jnp.max(scores, axis=-1)
    weights = jnp.exp(scores - top[..., None])
    total = jnp.sum(weights, axis=-1)
    summed = jnp.einsum(
        "hrs,she->rhe", weights.astype(jnp.bfloat16), values, preferred_element_type=jnp.float32
    )
    return (top.T, total.T, summed)


def select_rows(array, offsets, rate):
    rows = array.shape[0] // rate
    shaped = array.reshape(rows, rate, array.shape[1], array.shape[2])
    index = jnp.broadcast_to(
        offsets[None, None, :, None], (rows, 1, array.shape[1], array.shape[2])
    )
    return jnp.take_along_axis(shaped, index, axis=1)[:, 0]


def spread_rows(parts, offsets, rate):
    top, total, summed = parts
    rows = top.shape[0]
    marks = jnp.arange(rate, dtype=jnp.int32)[None, :, None] == offsets[None, None, :]
    top_full = jnp.where(marks, top[:, None, :], jnp.float32(-1e30)).reshape(rows * rate, -1)
    total_full = jnp.where(marks, total[:, None, :], jnp.float32(0.0)).reshape(rows * rate, -1)
    sum_full = jnp.where(marks[..., None], summed[:, None], jnp.float32(0.0)).reshape(
        rows * rate, summed.shape[1], summed.shape[2]
    )
    return (top_full, total_full, sum_full)


def body(tokens, w_qkv, w_out, norm_gain, w_label, offset_mid, offset_far):
    tok_rows = tokens.shape[0]
    local_heads = offset_mid.shape[0]
    head_size = w_qkv.shape[2] // local_heads
    qkv = jnp.einsum("td,dce->tce", tokens, w_qkv, preferred_element_type=jnp.float32).astype(
        jnp.bfloat16
    )
    qkv = qkv.reshape(tok_rows, 3, local_heads, head_size)
    queries, keys, values = (qkv[:, 0], qkv[:, 1], qkv[:, 2])
    seq_count = lax.axis_size("seq")
    near = attend(queries, keys, values)
    mid_q = select_rows(queries, offset_mid, SPAN)
    mid_kv = jnp.stack(
        [select_rows(keys, offset_mid, SPAN), select_rows(values, offset_mid, SPAN)], axis=0
    )
    mid_rows = mid_kv.shape[1]
    position = (lax.axis_index("seq") + SPAN // 2) % SPAN
    lower_pieces = []
    upper_pieces = []
    for step_back in range(1, SPAN):
        lower_pieces.insert(0, from_behind(mid_kv, "seq", step_back))
        upper_pieces.append(from_behind(mid_kv, "seq", -step_back))
    window = jnp.concatenate(lower_pieces + [mid_kv] + upper_pieces, axis=1)
    gathered = lax.dynamic_slice_in_dim(
        window, (SPAN - 1 - position) * mid_rows, SPAN * mid_rows, 1
    )
    middle = spread_rows(attend(mid_q, gathered[0], gathered[1]), offset_mid, SPAN)
    far_q = select_rows(queries, offset_far, seq_count)
    far_kv = jnp.stack(
        [select_rows(keys, offset_far, seq_count), select_rows(values, offset_far, seq_count)],
        axis=0,
    )
    far_all = lax.all_gather(far_kv, "seq", axis=1, tiled=True)
    distant = spread_rows(attend(far_q, far_all[0], far_all[1]), offset_far, seq_count)
    branches = [near, middle, distant]
    peak = jnp.maximum(jnp.maximum(near[0], middle[0]), distant[0])
    upper = jnp.zeros((tok_rows, local_heads, head_size), jnp.float32)
    lower = jnp.zeros((tok_rows, local_heads), jnp.float32)
    for top, total, summed in branches:
        factor = jnp.exp(top - peak)
        upper = upper + factor[..., None] * summed
        lower = lower + factor * total
    attn = (
        (upper / lower[..., None]).astype(jnp.bfloat16).reshape(tok_rows, local_heads * head_size)
    )
    partial_out = jnp.dot(attn, w_out, preferred_element_type=jnp.float32)
    projected = lax.psum(partial_out.astype(jnp.bfloat16), "head").astype(jnp.float32)
    mixed = tokens.astype(jnp.float32) + projected
    mean_sq = jnp.mean(mixed * mixed, axis=-1)
    scaled = (mixed * norm_gain).astype(jnp.bfloat16)
    product = jnp.dot(scaled, w_label, preferred_element_type=jnp.float32)
    return product / jnp.sqrt(mean_sq + 1e-05)[:, None]


def solution(mesh):
    return jax.shard_map(
        body,
        mesh=mesh,
        in_specs=(
            P("seq", None),
            P(None, None, "head"),
            P("head", None),
            P(),
            P(),
            P("head"),
            P("head"),
        ),
        out_specs=P("seq", None),
        check_vma=False,
    )
```

profile of v0, /device:TPU:32, one launch (start us, length us, event | category | flops | bytes accessed | tf_op | source)
XLA Modules:
  0.0 969.3 jit_solution(3699433661671569265)
XLA Ops:
  6.5 5.9 convolution_convert_fusion.1
  12.5 1.7 reshape.163
  16.3 235.5 %gather_fusion.1 = bf16[16384]{0:T(1024)(128)(2,1)} fusion(bf16[32,8,4,128]{3,1,0,2:T(8,128)(2,1)S(1)} %get-tuple-element.34, s32[16384]{0:T(1024)S(1)} %bitcast.149), kind=kCustom, calls=%fused_computation.2.clone | custom fusion | bytes 327680 | tf_op jit(solution)/shard_map/jit(take_along_axis)/gather | solution.py:34
  251.7 236.4 %gather_fusion.2 = bf16[16384]{0:T(1024)(128)(2,1)} fusion(bf16[32,8,4,128]{3,1,0,2:T(8,128)(2,1)S(1)} %get-tuple-element.20, s32[16384]{0:T(1024)S(1)} %bitcast.150), kind=kCustom, calls=%fused_computation.3.clone | custom fusion | bytes 327680 | tf_op jit(solution)/shard_map/jit(take_along_axis)/gather | solution.py:34
  489.6 5.3 collective-permute-start
  494.9 1.9 collective-permute-start.1
  497.9 4.5 collective-permute-start.3
  502.9 2.2 fusion.59
  507.2 236.0 %gather_fusion = bf16[16384]{0:T(1024)(128)(2,1)} fusion(bf16[32,8,4,128]{3,1,0,2:T(8,128)(2,1)S(1)} %bitcast.152, s32[16384]{0:T(1024)S(1)} %bitcast.151), kind=kCustom, calls=%fused_computation.clone | custom fusion | bytes 327680 | tf_op jit(solution)/shard_map/jit(take_along_axis)/gather | solution.py:34
  743.3 22.2 %gather_fusion.5 = bf16[2048]{0:T(1024)(128)(2,1)S(1)} fusion(bf16[4,64,4,128]{3,1,0,2:T(8,128)(2,1)S(1)} %bitcast.158, s32[2048]{0:T(1024)S(1)} %bitcast.154), kind=kCustom, calls=%fused_computation.5.clone | custom fusion | bytes 40960 | tf_op jit(solution)/shard_map/jit(take_along_axis)/gather | solution.py:34
  765.5 22.2 %gather_fusion.4 = bf16[2048]{0:T(1024)(128)(2,1)S(1)} fusion(bf16[4,64,4,128]{3,1,0,2:T(8,128)(2,1)S(1)} %bitcast.157, s32[2048]{0:T(1024)S(1)} %bitcast.155), kind=kCustom, calls=%fused_computation.4.clone | custom fusion | bytes 40960 | tf_op jit(solution)/shard_map/jit(take_along_axis)/gather | solution.py:34
  787.7 22.2 %gather_fusion.3 = bf16[2048]{0:T(1024)(128)(2,1)S(1)} fusion(bf16[4,64,4,128]{3,1,0,2:T(8,128)(2,1)S(1)} %bitcast.153, s32[2048]{0:T(1024)S(1)} %bitcast.156), kind=kCustom, calls=%fused_computation.1.clone | custom fusion | bytes 40960 | tf_op jit(solution)/shard_map/jit(take_along_axis)/gather | solution.py:34
  810.0 49.2 %all_gather.3 = bf16[2,256,4,128]{3,2,0,1:T(4,128)(2,1)S(1)} all-gather(bf16[2,4,4,128]{3,2,0,1:T(4,128)(2,1)S(1)} %copy.67), channel_id=1, replica_groups=mesh['seq'=64,'head'=4] {'seq'}, dimensions={1}, use_global_device_ids=true | all-gather | bytes 532480 | tf_op jit(solution)/shard_map/all_gather | solution.py:81
  864.0 2.0 copy.73
  868.4 1.8 collective-permute-start.7
  871.0 5.0 collective-permute-start.8
  880.5 4.9 collective-permute-start.12
  887.8 3.2 collective-permute-done.11
  891.1 7.0 collective-permute-done.13
  902.7 2.0 copy.71
  907.1 1.7 convolution_convert_fusion
  908.9 49.1 %all-reduce.2.cloned.1.call-done = bf16[256,2048]{1,0:T(8,128)(2,1)} async-done(((bf16[256,2048]{1,0:T(8,128)(2,1)}), bf16[256,2048]{1,0:T(8,128)(2,1)}) %all-reduce.2.cloned.1.call-update) | async-done | bytes 1048592 | tf_op jit(solution)/shard_map/psum | solution.py:95
  958.0 2.0 multiply_reduce_fusion
  960.0 2.5 convolution_divide_fusion
  (113 shorter events, 29.2 us)
Async XLA Ops:
  6.5 900.6 %copy-start = (bf16[512,2048]{1,0:T(8,128)(2,1)S(1)}, bf16[512,2048]{1,0:T(8,128)(2,1)}, u32[]{:S(2)}) copy-start(bf16[512,2048]{1,0:T(8,128)(2,1)} %param.13) | copy-start | bytes 6291460
  6.5 8.7 copy-start.9
  6.5 951.4 %all-reduce.2.cloned.1.call-start = ((), (), s32[]{:S(2)}) async-start(), calls=%async_computation | async-start | bytes 2097152 | tf_op jit(solution)/shard_map/psum | solution.py:95
  15.2 472.9 %copy-start.8 = (s32[4]{0:T(128)}, s32[4]{0:T(128)S(1)}, u32[]{:S(2)}) copy-start(s32[4]{0:T(128)S(1)} %broadcast_add_fusion.1) | copy-start | bytes 52
  15.8 472.3 %copy-start.7 = (pred[4]{0:T(512)(128)(4,1)}, pred[4]{0:T(512)(128)(4,1)S(1)}, u32[]{:S(2)}) copy-start(pred[4]{0:T(512)(128)(4,1)S(1)} %get-tuple-element.36) | copy-start | bytes 16
  251.7 251.1 %copy-start.2 = (bf16[256,1,4,128]{3,2,0,1:T(4,128)(2,1)S(1)}, bf16[256,1,4,128]{3,2,0,1:T(4,128)(2,1)}, u32[]{:S(2)}) copy-start(bf16[256,1,4,128]{3,2,0,1:T(4,128)(2,1)} %get-tuple-element.12) | copy-start | bytes 786436
  489.6 376.5 %collective-permute-start = (bf16[2,32,4,128]{3,1,2,0:T(8,128)(2,1)}, bf16[2,32,4,128]{3,1,2,0:T(8,128)(2,1)}, u32[]{:S(2)}, u32[]{:S(2)}) collective-permute-start(bf16[2,32,4,128]{3,1,2,0:T(8,128)(2,1)} %pad_maximum_fusion), channel_id=1, source_target_pairs={{228,0},{232,4},{236,8},{240,12},{244,16},{248,20},{252,24},{0,28}... | collective-permute-start | bytes 196616 | tf_op jit(solution)/shard_map/ppermute | solution.py:12
  494.9 372.5 %collective-permute-start.1 = (bf16[2,32,4,128]{3,1,2,0:T(8,128)(2,1)}, bf16[2,32,4,128]{3,1,2,0:T(8,128)(2,1)}, u32[]{:S(2)}, u32[]{:S(2)}) collective-permute-start(bf16[2,32,4,128]{3,1,2,0:T(8,128)(2,1)} %pad_maximum_fusion), channel_id=1, source_target_pairs={{232,0},{236,4},{240,8},{244,12},{248,16},{252,20},{0,24},{4,28},{... | collective-permute-start | bytes 196616 | tf_op jit(solution)/shard_map/ppermute | solution.py:12
  496.8 371.6 %collective-permute-start.2 = (bf16[2,32,4,128]{3,1,2,0:T(8,128)(2,1)}, bf16[2,32,4,128]{3,1,2,0:T(8,128)(2,1)}, u32[]{:S(2)}, u32[]{:S(2)}) collective-permute-start(bf16[2,32,4,128]{3,1,2,0:T(8,128)(2,1)} %pad_maximum_fusion), channel_id=1, source_target_pairs={{236,0},{240,4},{244,8},{248,12},{252,16},{0,20},{4,24},{8,28},{12... | collective-permute-start | bytes 196616 | tf_op jit(solution)/shard_map/ppermute | solution.py:12
  497.9 373.1 %collective-permute-start.3 = (bf16[2,32,4,128]{3,1,2,0:T(8,128)(2,1)}, bf16[2,32,4,128]{3,1,2,0:T(8,128)(2,1)}, u32[]{:S(2)}, u32[]{:S(2)}) collective-permute-start(bf16[2,32,4,128]{3,1,2,0:T(8,128)(2,1)} %pad_maximum_fusion), channel_id=1, source_target_pairs={{240,0},{244,4},{248,8},{252,12},{0,16},{4,20},{8,24},{12,28},{16,... | collective-permute-start | bytes 196616 | tf_op jit(solution)/shard_map/ppermute | solution.py:12
  502.4 374.4 %collective-permute-start.4 = (bf16[2,32,4,128]{3,1,2,0:T(8,128)(2,1)}, bf16[2,32,4,128]{3,1,2,0:T(8,128)(2,1)}, u32[]{:S(2)}, u32[]{:S(2)}) collective-permute-start(bf16[2,32,4,128]{3,1,2,0:T(8,128)(2,1)} %pad_maximum_fusion), channel_id=1, source_target_pairs={{244,0},{248,4},{252,8},{0,12},{4,16},{8,20},{12,24},{16,28},{20,3... | collective-permute-start | bytes 196616 | tf_op jit(solution)/shard_map/ppermute | solution.py:12
  507.2 236.0 %copy-start.10 = (pred[4]{0:T(512)(128)(4,1)S(1)}, pred[4]{0:T(512)(128)(4,1)}, u32[]{:S(2)}) copy-start(pred[4]{0:T(512)(128)(4,1)} %get-tuple-element.35) | copy-start | bytes 16
  787.7 72.0 %copy-start.1 = (f32[4,256,256]{1,2,0:T(8,128)S(1)}, f32[4,256,256]{1,2,0:T(8,128)}, u32[]{:S(2)}) copy-start(f32[4,256,256]{1,2,0:T(8,128)} %get-tuple-element.32) | copy-start | bytes 3145732
  866.0 12.5 %collective-permute-start.5 = (bf16[2,32,4,128]{3,1,2,0:T(8,128)(2,1)}, bf16[2,32,4,128]{3,1,2,0:T(8,128)(2,1)S(1)}, u32[]{:S(2)}, u32[]{:S(2)}) collective-permute-start(bf16[2,32,4,128]{3,1,2,0:T(8,128)(2,1)} %pad_maximum_fusion), channel_id=1, source_target_pairs={{248,0},{252,4},{0,8},{4,12},{8,16},{12,20},{16,24},{20,28},{24,32... | collective-permute-start | bytes 196616 | tf_op jit(solution)/shard_map/ppermute | solution.py:12
  867.4 11.6 %collective-permute-start.6 = (bf16[2,32,4,128]{3,1,2,0:T(8,128)(2,1)}, bf16[2,32,4,128]{3,1,2,0:T(8,128)(2,1)S(1)}, u32[]{:S(2)}, u32[]{:S(2)}) collective-permute-start(bf16[2,32,4,128]{3,1,2,0:T(8,128)(2,1)} %pad_maximum_fusion), channel_id=1, source_target_pairs={{252,0},{0,4},{4,8},{8,12},{12,16},{16,20},{20,24},{24,28},{28,32}... | collective-permute-start | bytes 196616 | tf_op jit(solution)/shard_map/ppermute | solution.py:12
  868.4 12.1 %collective-permute-start.7 = (bf16[2,32,4,128]{3,1,2,0:T(8,128)(2,1)}, bf16[2,32,4,128]{3,1,2,0:T(8,128)(2,1)S(1)}, u32[]{:S(2)}, u32[]{:S(2)}) collective-permute-start(bf16[2,32,4,128]{3,1,2,0:T(8,128)(2,1)} %pad_maximum_fusion), channel_id=1, source_target_pairs={{4,0},{8,4},{12,8},{16,12},{20,16},{24,20},{28,24},{32,28},{36,32}... | collective-permute-start | bytes 196616 | tf_op jit(solution)/shard_map/ppermute | solution.py:12
  871.0 14.5 %collective-permute-start.8 = (bf16[2,32,4,128]{3,1,2,0:T(8,128)(2,1)}, bf16[2,32,4,128]{3,1,2,0:T(8,128)(2,1)S(1)}, u32[]{:S(2)}, u32[]{:S(2)}) collective-permute-start(bf16[2,32,4,128]{3,1,2,0:T(8,128)(2,1)} %pad_maximum_fusion), channel_id=1, source_target_pairs={{8,0},{12,4},{16,8},{20,12},{24,16},{28,20},{32,24},{36,28},{40,32... | collective-permute-start | bytes 196616 | tf_op jit(solution)/shard_map/ppermute | solution.py:12
  876.8 9.3 collective-permute-start.9
  878.6 9.2 collective-permute-start.10
  879.0 12.1 %collective-permute-start.11 = (bf16[2,32,4,128]{3,1,2,0:T(8,128)(2,1)}, bf16[2,32,4,128]{3,1,2,0:T(8,128)(2,1)S(1)}, u32[]{:S(2)}, u32[]{:S(2)}) collective-permute-start(bf16[2,32,4,128]{3,1,2,0:T(8,128)(2,1)} %pad_maximum_fusion), channel_id=1, source_target_pairs={{20,0},{24,4},{28,8},{32,12},{36,16},{40,20},{44,24},{48,28},{52,3... | collective-permute-start | bytes 196616 | tf_op jit(solution)/shard_map/ppermute | solution.py:12
  880.5 10.6 %collective-permute-start.12 = (bf16[2,32,4,128]{3,1,2,0:T(8,128)(2,1)}, bf16[2,32,4,128]{3,1,2,0:T(8,128)(2,1)S(1)}, u32[]{:S(2)}, u32[]{:S(2)}) collective-permute-start(bf16[2,32,4,128]{3,1,2,0:T(8,128)(2,1)} %pad_maximum_fusion), channel_id=1, source_target_pairs={{24,0},{28,4},{32,8},{36,12},{40,16},{44,20},{48,24},{52,28},{56,3... | collective-permute-start | bytes 196616 | tf_op jit(solution)/shard_map/ppermute | solution.py:12
  885.4 12.6 %collective-permute-start.13 = (bf16[2,32,4,128]{3,1,2,0:T(8,128)(2,1)}, bf16[2,32,4,128]{3,1,2,0:T(8,128)(2,1)S(1)}, u32[]{:S(2)}, u32[]{:S(2)}) collective-permute-start(bf16[2,32,4,128]{3,1,2,0:T(8,128)(2,1)} %pad_maximum_fusion), channel_id=1, source_target_pairs={{28,0},{32,4},{36,8},{40,12},{44,16},{48,20},{52,24},{56,28},{60,3... | collective-permute-start | bytes 196616 | tf_op jit(solution)/shard_map/ppermute | solution.py:12
  900.6 59.3 %copy-start.11 = (f32[2048]{0:T(1024)S(1)}, f32[2048]{0:T(1024)}, u32[]{:S(2)}) copy-start(f32[2048]{0:T(1024)} %param.14) | copy-start | bytes 24580
  907.1 52.8 %copy-start.4 = (bf16[256,2048]{1,0:T(8,128)(2,1)S(1)}, bf16[256,2048]{1,0:T(8,128)(2,1)}, u32[]{:S(2)}) copy-start(bf16[256,2048]{1,0:T(8,128)(2,1)} %param.11) | copy-start | bytes 3145732
  (3 other events, 10.5 us)
Sparse Core Ops, SparseCore 0:
  909.0 48.9 all-reduce.1
where the time goes:
time: 970 us; the launch traced here: 969 us
  local copies, waits for them, and re-layouts  793 us (82%)
  waiting for transfers between devices  61 us (6%)
  blocking collectives  49.2 us (5%)
  starting transfers between devices  28.9 us (3%)
  matrix products  16.8 us (2%)
  between operations  13.8 us (1%)
    gather x7, local copies, waits for them, and re-layouts, select_rows(): return jnp.take_along_axis(shaped, index, axis=1)[:, 0]  774 us
    all_gather x1, blocking collectives, body(): far_all = lax.all_gather(far_kv, 'seq', axis=1, tiled=True)  49.2 us
    psum x1, waiting for transfers between devices, body(): lax.psum(partial_out.astype(jnp.bfloat16), 'head').astype(jnp.float32)  49.1 us
    ppermute x14, starting transfers between devices, from_behind(): return lax.ppermute(block, axis, route)  28.9 us
  transfers between devices with their start and end apart: 15, of which 4 were waited for; matrix products, arithmetic and copies ran while one was open for 33% of the time, Pallas kernels for 0%

commit v1 on v0

v1 whole, which is shorter than its diff:
```python
import jax
import jax.numpy as jnp
from jax import lax
from jax.sharding import PartitionSpec as P

SPAN = 8


def segments(seq_count):
    return [
        [(SPAN * k - SPAN // 2 + i) % seq_count for i in range(SPAN)]
        for k in range(seq_count // SPAN)
    ]


def share(block, axis, groups):
    pieces = [block]
    for step in range(1, len(groups[0])):
        route = [(g[i], g[i ^ step]) for g in groups for i in range(len(g))]
        pieces.append(lax.ppermute(block, axis, route))
    return jnp.stack(pieces)


def attend(queries, keys, values):
    scores = jnp.einsum(
        "hre,hse->hrs", queries, keys, preferred_element_type=jnp.float32
    ) / jnp.sqrt(jnp.float32(queries.shape[2]))
    top = jnp.max(scores, axis=-1, keepdims=True)
    weights = jnp.exp(scores - top)
    total = jnp.sum(weights, axis=-1, keepdims=True)
    summed = jnp.einsum(
        "hrs,hse->hre", weights.astype(jnp.bfloat16), values, preferred_element_type=jnp.float32
    )
    return (top, total, summed)


def pick(offsets, rows, rate):
    where = jnp.arange(rows // rate, dtype=jnp.int32)[None, :, None] * rate
    where = where + offsets[:, None, None]
    return where == jnp.arange(rows, dtype=jnp.int32)[None, None, :]


def take(marks, array):
    return jnp.einsum(
        "hjr,hre->hje",
        marks.astype(jnp.bfloat16),
        array,
        preferred_element_type=jnp.float32,
    ).astype(jnp.bfloat16)


def spread(marks, parts):
    top, total, summed = parts
    hit = jnp.any(marks, axis=1)[..., None]
    put = lambda a: jnp.einsum(
        "hjr,hje->hre", marks.astype(jnp.float32), a, precision=lax.Precision.HIGHEST
    )
    return (jnp.where(hit, put(top), jnp.float32(-1e30)), put(total), put(summed))


def body(tokens, w_qkv, w_out, norm_gain, w_label, offset_mid, offset_far):
    tok_rows, width = tokens.shape
    local_heads = offset_mid.shape[0]
    head_size = w_qkv.shape[2] // local_heads
    seq_count = lax.axis_size("seq")
    head_count = lax.axis_size("head")
    split = lambda a: a.reshape(tok_rows, local_heads, head_size).transpose(1, 0, 2)
    qkv = [
        split(
            jnp.dot(tokens, w_qkv[:, c], preferred_element_type=jnp.float32).astype(jnp.bfloat16)
        )
        for c in range(3)
    ]
    queries, keys, values = qkv

    groups = segments(seq_count)
    across = [[g[2 * i + c] for i in range(SPAN // 2)] for g in groups for c in range(2)]
    cores = [[2 * i, 2 * i + 1] for i in range(seq_count // 2)]
    along_z = [[16 * y + 2 * z + c for z in range(8)] for y in range(4) for c in range(2)]
    along_y = [[16 * y + r for y in range(4)] for r in range(16)]

    mid_marks = pick(offset_mid, tok_rows, SPAN)
    far_marks = pick(offset_far, tok_rows, seq_count)
    mid_kv = jnp.stack([take(mid_marks, keys), take(mid_marks, values)])
    far_kv = jnp.stack([take(far_marks, keys), take(far_marks, values)])
    mid_all = share(share(mid_kv, "seq", across), "seq", cores)
    far_all = share(share(share(far_kv, "seq", along_z), "seq", along_y), "seq", cores)
    gather = lambda a: jnp.moveaxis(
        a.reshape((-1,) + a.shape[-4:]), 0, 2
    ).reshape(2, local_heads, -1, head_size)
    mid_all = gather(mid_all)
    far_all = gather(far_all)

    near = attend(queries, keys, values)
    middle = spread(mid_marks, attend(take(mid_marks, queries), mid_all[0], mid_all[1]))
    distant = spread(far_marks, attend(take(far_marks, queries), far_all[0], far_all[1]))
    branches = [near, middle, distant]
    peak = jnp.maximum(jnp.maximum(near[0], middle[0]), distant[0])
    upper = sum(jnp.exp(top - peak) * summed for top, total, summed in branches)
    lower = sum(jnp.exp(top - peak) * total for top, total, summed in branches)
    attn = (upper / lower).astype(jnp.bfloat16)
    attn = attn.transpose(1, 0, 2).reshape(tok_rows, local_heads * head_size)
    part = jnp.dot(attn, w_out, preferred_element_type=jnp.float32).astype(jnp.bfloat16)

    place = lax.axis_index("head")
    own_rows = tok_rows // head_count
    quarter = lambda a, i: lax.dynamic_slice_in_dim(a, i * own_rows, own_rows, 0)
    mixed = quarter(tokens, place).astype(jnp.float32) + quarter(part, place).astype(jnp.float32)
    for step in range(1, head_count):
        route = [(i, i ^ step) for i in range(head_count)]
        mixed = mixed + lax.ppermute(quarter(part, place ^ step), "head", route).astype(
            jnp.float32
        )
    mean_sq = jnp.mean(mixed * mixed, axis=-1)
    scaled = (mixed * norm_gain).astype(jnp.bfloat16)
    product = jnp.dot(scaled, w_label, preferred_element_type=jnp.float32)
    own = product / jnp.sqrt(mean_sq + 1e-05)[:, None]
    logits = jnp.zeros((head_count,) + own.shape, jnp.float32)
    every = share(own, "head", [list(range(head_count))])
    for step in range(head_count):
        logits = lax.dynamic_update_index_in_dim(logits, every[step], place ^ step, 0)
    return logits.reshape(tok_rows, -1)


def solution(mesh):
    return jax.shard_map(
        body,
        mesh=mesh,
        in_specs=(
            P("seq", None),
            P(None, None, "head"),
            P("head", None),
            P(),
            P(),
            P("head"),
            P("head"),
        ),
        out_specs=P("seq", None),
        check_vma=False,
    )
```

time: 970 us -> 97 us (0.10)
  local copies, waits for them, and re-layouts: 793 us -> 4.04 us
  blocking collectives: 49.2 us -> 0 us
  waiting for transfers between devices: 61 us -> 20.4 us
  between operations: 13.8 us -> 0.39 us
  starting transfers between devices: 28.9 us -> 38.7 us
    gather x7 -> x0, local copies, waits for them, and re-layouts: 774 us -> none  [select_rows(): return jnp.take_along_axis(shaped, index, axis=1)[:, 0]]
    all_gather x1 -> x0, blocking collectives: 49.2 us -> none  [body(): far_all = lax.all_gather(far_kv, 'seq', axis=1, tiled=True)]
    psum x1 -> x0, waiting for transfers between devices: 49.1 us -> none  [body(): lax.psum(partial_out.astype(jnp.bfloat16), 'head').astype(jnp.float32)]
    ppermute x14 -> x21, starting transfers between devices: 28.9 us -> 38.7 us  [the longest x18 34 us: share(): pieces.append(lax.ppermute(block, axis, route))]
    ppermute x14 -> x21, waiting for transfers between devices: 11.9 us -> 20.4 us  [the longest x3 14.3 us: body(): lax.ppermute(quarter(part, place ^ step), 'head', route).astype(jnp.float32)]
    dot_general x8 -> x20, matrix products: 14.2 us -> 19.7 us  [the longest x3 7.69 us: body(): jnp.dot(tokens, w_qkv[:, c], preferred_element_type=jnp.float32)]
  transfers between devices with their start and end apart: 15 -> 21, of which waited for: 4 -> 6; matrix products, arithmetic and copies ran while one was open for 33% -> 19% of each run, Pallas kernels for 0% -> 0%
where the time goes in v1:
time: 97 us; the launch traced here: 96.5 us
  starting transfers between devices  38.7 us (40%)
  matrix products  21.9 us (23%)
  waiting for transfers between devices  20.4 us (21%)
  other arithmetic  11.1 us (11%)
  local copies, waits for them, and re-layouts  4.04 us (4%)
    ppermute x18, starting transfers between devices, share(): pieces.append(lax.ppermute(block, axis, route))  34 us
    ppermute x3, waiting for transfers between devices, body(): lax.ppermute(quarter(part, place ^ step), 'head', route).astype(jnp.float32)  14.3 us
    dot_general x3, matrix products, body(): jnp.dot(tokens, w_qkv[:, c], preferred_element_type=jnp.float32)  7.69 us
    another operation x6, other arithmetic, share(): return jnp.stack(pieces)  7.01 us
    ppermute x18, waiting for transfers between devices, share(): pieces.append(lax.ppermute(block, axis, route))  6.11 us
    ppermute x3, starting transfers between devices, body(): lax.ppermute(quarter(part, place ^ step), 'head', route).astype(jnp.float32)  4.7 us
    dot_general x3, matrix products, attend(): jnp.einsum('hre,hse->hrs', queries, keys, preferred_element_type=jnp.floa...  4.15 us
    dot_general x3, matrix products, attend(): jnp.einsum('hrs,hse->hre', weights.astype(jnp.bfloat16), values, preferre...  3.28 us
  transfers between devices with their start and end apart: 21, of which 6 were waited for; matrix products, arithmetic and copies ran while one was open for 19% of the time, Pallas kernels for 0%

profile of v1, /device:TPU:32, one launch (start us, length us, event | category | flops | bytes accessed | tf_op | source)
XLA Modules:
  0.0 96.5 jit_solution(10008525808192565936)
XLA Ops:
  0.0 2.8 %fusion.22 = bf16[256,512]{1,0:T(8,128)(2,1)S(1)} fusion(bf16[256,2048]{1,0:T(8,128)(2,1)} %param.7, bf16[2048,3,512]{2,0,1:T(8,128)(2,1)} %param.8), kind=kOutput, calls=%fused_computation.23 | convolution fusion | flops 537001984 | bytes 3407872 | tf_op jit(solution)/shard_map/dot_general | solution.py:70
  2.8 2.3 %fusion.25 = bf16[32,4,8,128]{3,2,1,0:T(8,128)(2,1)S(1)} fusion(bf16[256,2048]{1,0:T(8,128)(2,1)S(1)} %copy-done.3, bf16[2048,3,512]{2,0,1:T(8,128)(2,1)} %param.8), kind=kOutput, calls=%fused_computation.24 | convolution fusion | flops 537001984 | bytes 3407872 | tf_op jit(solution)/shard_map/dot_general | solution.py:70
  5.8 1.9 %collective-permute-start.4 = (bf16[2,4,4,128]{3,2,1,0:T(4,128)(2,1)S(1)}, bf16[2,4,4,128]{3,2,1,0:T(4,128)(2,1)S(1)}, u32[]{:S(2)}, u32[]{:S(2)}) collective-permute-start(bf16[2,4,4,128]{3,2,1,0:T(4,128)(2,1)S(1)} %pad_maximum_fusion.5), channel_id=1, source_target_pairs={{0,8},{8,0},{16,24},{24,16},{32,40},{40,32},{48,56},{56,48},{4,12}... | collective-permute-start | bytes 24584 | tf_op jit(solution)/shard_map/ppermute | solution.py:20
  7.7 1.6 %collective-permute-start.5 = (bf16[2,4,4,128]{3,2,1,0:T(4,128)(2,1)S(1)}, bf16[2,4,4,128]{3,2,1,0:T(4,128)(2,1)S(1)}, u32[]{:S(2)}, u32[]{:S(2)}) collective-permute-start(bf16[2,4,4,128]{3,2,1,0:T(4,128)(2,1)S(1)} %pad_maximum_fusion.5), channel_id=1, source_target_pairs={{0,16},{8,24},{16,0},{24,8},{32,48},{40,56},{48,32},{56,40},{4,20}... | collective-permute-start | bytes 24584 | tf_op jit(solution)/shard_map/ppermute | solution.py:20
  9.7 5.9 %collective-permute-start.7 = (bf16[2,4,4,128]{3,2,1,0:T(4,128)(2,1)S(1)}, bf16[2,4,4,128]{3,2,1,0:T(4,128)(2,1)S(1)}, u32[]{:S(2)}, u32[]{:S(2)}) collective-permute-start(bf16[2,4,4,128]{3,2,1,0:T(4,128)(2,1)S(1)} %pad_maximum_fusion.5), channel_id=1, source_target_pairs={{0,32},{8,40},{16,48},{24,56},{32,0},{40,8},{48,16},{56,24},{4,36}... | collective-permute-start | bytes 24584 | tf_op jit(solution)/shard_map/ppermute | solution.py:20
  16.6 2.6 %fusion.28 = bf16[32,4,8,128]{3,2,1,0:T(8,128)(2,1)S(1)} fusion(bf16[256,2048]{1,0:T(8,128)(2,1)} %param.7, bf16[2048,3,512]{2,0,1:T(8,128)(2,1)} %param.8), kind=kOutput, calls=%fused_computation.25 | convolution fusion | flops 537001984 | bytes 3407872 | tf_op jit(solution)/shard_map/dot_general | solution.py:70
  22.5 3.8 %collective-permute-start.9 = (bf16[2,4,4,128]{3,2,1,0:T(4,128)(2,1)S(1)}, bf16[2,4,4,128]{3,2,1,0:T(4,128)(2,1)S(1)}, u32[]{:S(2)}, u32[]{:S(2)}) collective-permute-start(bf16[2,4,4,128]{3,2,1,0:T(4,128)(2,1)S(1)} %pad_maximum_fusion.5), channel_id=1, source_target_pairs={{0,48},{8,56},{16,32},{24,40},{32,16},{40,24},{48,0},{56,8},{4,52}... | collective-permute-start | bytes 24584 | tf_op jit(solution)/shard_map/ppermute | solution.py:20
  26.3 1.5 %collective-permute-start.10 = (bf16[2,4,4,128]{3,2,1,0:T(4,128)(2,1)S(1)}, bf16[2,4,4,128]{3,2,1,0:T(4,128)(2,1)S(1)}, u32[]{:S(2)}, u32[]{:S(2)}) collective-permute-start(bf16[2,4,4,128]{3,2,1,0:T(4,128)(2,1)S(1)} %pad_maximum_fusion.5), channel_id=1, source_target_pairs={{0,56},{8,48},{16,40},{24,32},{32,24},{40,16},{48,8},{56,0},{4,60}... | collective-permute-start | bytes 24584 | tf_op jit(solution)/shard_map/ppermute | solution.py:20
  28.4 6.2 %collective-permute-start.1 = (bf16[2,4,32,128]{3,2,1,0:T(8,128)(2,1)S(1)}, bf16[2,4,32,128]{3,2,1,0:T(8,128)(2,1)S(1)}, u32[]{:S(2)}, u32[]{:S(2)}) collective-permute-start(bf16[2,4,32,128]{3,2,1,0:T(8,128)(2,1)S(1)} %get-tuple-element.19), channel_id=1, source_target_pairs={{240,0},{248,8},{0,240},{8,248},{244,4},{252,12},{4,244},{12,252},... | collective-permute-start | bytes 196616 | tf_op jit(solution)/shard_map/ppermute | solution.py:20
  36.3 2.9 %collective-permute-start.12 = (bf16[8,2,4,4,128]{4,3,2,1,0:T(4,128)(2,1)S(1)}, bf16[8,2,4,4,128]{4,3,2,1,0:T(4,128)(2,1)}, u32[]{:S(2)}, u32[]{:S(2)}) collective-permute-start(bf16[8,2,4,4,128]{4,3,2,1,0:T(4,128)(2,1)S(1)} %constant_dynamic-update-slice_fusion), channel_id=1, source_target_pairs={{0,128},{64,192},{128,0},{192,64},{4,132},{68,196},{132,4},{196,68... | collective-permute-start | bytes 196616 | tf_op jit(solution)/shard_map/ppermute | solution.py:20
  40.6 3.5 %collective-permute-done.2 = bf16[2,4,32,128]{3,2,1,0:T(8,128)(2,1)S(1)} collective-permute-done((bf16[2,4,32,128]{3,2,1,0:T(8,128)(2,1)S(1)}, bf16[2,4,32,128]{3,2,1,0:T(8,128)(2,1)S(1)}, u32[]{:S(2)}, u32[]{:S(2)}) %collective-permute-start.2) | collective-permute-done | bytes 65568 | tf_op jit(solution)/shard_map/ppermute | solution.py:20
  45.7 1.8 %pad_maximum_fusion.3 = bf16[4,8,2,4,4,128]{5,4,3,2,1,0:T(4,128)(2,1)} fusion(bf16[1,8,2,4,4,128]{5,4,3,2,1,0:T(4,128)(2,1)} %bitcast.37, bf16[1,8,2,4,4,128]{5,4,3,2,1,0:T(4,128)(2,1)} %bitcast.36, bf16[1,8,2,4,4,128]{5,4,3,2,1,0:T(4,128)(2,1)S(1)} %bitcast.282, bf16[1,8,2,4,4,128]{5,4,3,2,1,0:T(4,128)(2,1)S(1)} %bitcast.278), kind=kLoop, calls=%fused_computation.53 | loop fusion | flops 393216 | bytes 524288 | tf_op jit(solution)/shard_map/stack | solution.py:21
  48.0 1.8 %fusion.112 = bf16[1,4,8,2,4,4,128]{6,5,4,3,2,1,0:T(4,128)(2,1)} fusion(bf16[1,8,2,4,4,128]{5,4,3,2,1,0:T(4,128)(2,1)} %bitcast.37, bf16[1,8,2,4,4,128]{5,4,3,2,1,0:T(4,128)(2,1)} %bitcast.36, bf16[1,8,2,4,4,128]{5,4,3,2,1,0:T(4,128)(2,1)S(1)} %bitcast.283, bf16[1,8,2,4,4,128]{5,4,3,2,1,0:T(4,128)(2,1)S(1)} %bitcast.279), kind=kLoop, calls=%fused_computation.135 | loop fusion | flops 393216 | bytes 524288 | tf_op jit(solution)/shard_map/stack | solution.py:21
  51.8 1.5 %fusion.90 = (f32[4,32]{1,0:T(4,128)S(1)}, f32[4,32,256]{2,1,0:T(8,128)S(1)}) fusion(bf16[4,256,128]{2,1,0:T(8,128)(2,1)} %bitcast.277, bf16[32,4,8,128]{3,2,1,0:T(8,128)(2,1)} %copy-done.1, s32[4,32]{1,0:T(4,128)S(1)} %broadcast_add_fusion.1), kind=kOutput, calls=%fused_computation.132 | convolution fusion | flops 16891776 | bytes 656384 | tf_op jit(solution)/shard_map/hre,hse->hrs/dot_general | solution.py:25
  55.1 1.8 %fusion.53 = f32[4,32,128]{2,1,0:T(8,128)} fusion(bf16[4,256,128]{2,1,0:T(8,128)(2,1)} %bitcast.275, f32[4,32,256]{2,1,0:T(8,128)S(1)} %get-tuple-element.21, f32[4,32]{1,0:T(4,128)S(1)} %get-tuple-element.20), kind=kOutput, calls=%fused_computation.68 | convolution fusion | flops 8454144 | bytes 459264 | tf_op jit(solution)/shard_map/hrs,hse->hre/dot_general | solution.py:31
  65.9 1.5 %collective-permute-start.15 = (bf16[64,2048]{1,0:T(8,128)(2,1)}, bf16[64,2048]{1,0:T(8,128)(2,1)S(1)}, u32[]{:S(2)}, u32[]{:S(2)}) collective-permute-start(bf16[64,2048]{1,0:T(8,128)(2,1)} %get-tuple-element.9), channel_id=1, source_target_pairs={{0,1},{1,0},{2,3},{3,2},{4,5},{5,4},{6,7},{7,6},{8,9},{9,8},{10,11... | collective-permute-start | bytes 786440 | tf_op jit(solution)/shard_map/ppermute | solution.py:111
  67.4 2.7 %collective-permute-start.16 = (bf16[64,2048]{1,0:T(8,128)(2,1)}, bf16[64,2048]{1,0:T(8,128)(2,1)}, u32[]{:S(2)}, u32[]{:S(2)}) collective-permute-start(bf16[64,2048]{1,0:T(8,128)(2,1)} %get-tuple-element.11), channel_id=1, source_target_pairs={{0,2},{1,3},{2,0},{3,1},{4,6},{5,7},{6,4},{7,5},{8,10},{9,11},{10,... | collective-permute-start | bytes 786440 | tf_op jit(solution)/shard_map/ppermute | solution.py:111
  70.6 4.7 %collective-permute-done.15 = bf16[64,2048]{1,0:T(8,128)(2,1)S(1)} collective-permute-done((bf16[64,2048]{1,0:T(8,128)(2,1)}, bf16[64,2048]{1,0:T(8,128)(2,1)S(1)}, u32[]{:S(2)}, u32[]{:S(2)}) %collective-permute-start.15) | collective-permute-done | bytes 262176 | tf_op jit(solution)/shard_map/ppermute | solution.py:111
  75.3 7.1 %collective-permute-done.16 = bf16[64,2048]{1,0:T(8,128)(2,1)} collective-permute-done((bf16[64,2048]{1,0:T(8,128)(2,1)}, bf16[64,2048]{1,0:T(8,128)(2,1)}, u32[]{:S(2)}, u32[]{:S(2)}) %collective-permute-start.16) | collective-permute-done | bytes 262176 | tf_op jit(solution)/shard_map/ppermute | solution.py:111
  82.4 2.6 %collective-permute-done.17 = bf16[64,2048]{1,0:T(8,128)(2,1)} collective-permute-done((bf16[64,2048]{1,0:T(8,128)(2,1)}, bf16[64,2048]{1,0:T(8,128)(2,1)}, u32[]{:S(2)}, u32[]{:S(2)}) %collective-permute-start.17) | collective-permute-done | bytes 262176 | tf_op jit(solution)/shard_map/ppermute | solution.py:111
  86.4 2.2 %bitcast_dynamic-update-slice_fusion.3 = (f32[4,64,128]{2,1,0:T(8,128)S(1)}, f32[64,128]{1,0:T(8,128)}) fusion(f32[4,64,128]{2,1,0:T(8,128)S(1)} %broadcast_in_dim.19, s32[]{:T(128)S(6)} %select_n.57, f32[64]{0:T(128)S(1)} %add_sqrt_fusion, bf16[2048,128]{1,0:T(8,128)(2,1)} %param.11, f32[2048]{0:T(1024)S(1)} %copy-done.7, ...), kind=kOutput, calls=%fused_computation.80 | convolution fusion | flops 35004416 | bytes 1909256 | tf_op jit(solution)/shard_map/dot_general | solution.py:116
  88.6 1.9 %collective-permute-start.19 = (f32[64,128]{1,0:T(8,128)}, f32[64,128]{1,0:T(8,128)S(1)}, u32[]{:S(2)}, u32[]{:S(2)}) collective-permute-start(f32[64,128]{1,0:T(8,128)} %get-tuple-element.27), channel_id=1, source_target_pairs={{0,2},{1,3},{2,0},{3,1},{4,6},{5,7},{6,4},{7,5},{8,10},{9,11},{10,... | collective-permute-start | bytes 98312 | tf_op jit(solution)/shard_map/ppermute | solution.py:20
  90.5 2.8 %collective-permute-start.20 = (f32[64,128]{1,0:T(8,128)}, f32[64,128]{1,0:T(8,128)S(1)}, u32[]{:S(2)}, u32[]{:S(2)}) collective-permute-start(f32[64,128]{1,0:T(8,128)} %get-tuple-element.27), channel_id=1, source_target_pairs={{0,3},{1,2},{2,1},{3,0},{4,7},{5,6},{6,5},{7,4},{8,11},{9,10},{10,... | collective-permute-start | bytes 98312 | tf_op jit(solution)/shard_map/ppermute | solution.py:20
  94.2 1.6 %collective-permute-done.20 = f32[64,128]{1,0:T(8,128)S(1)} collective-permute-done((f32[64,128]{1,0:T(8,128)}, f32[64,128]{1,0:T(8,128)S(1)}, u32[]{:S(2)}, u32[]{:S(2)}) %collective-permute-start.20) | collective-permute-done | bytes 32800 | tf_op jit(solution)/shard_map/ppermute | solution.py:20
  (104 shorter events, 27.2 us)
Async XLA Ops:
  0.0 64.2 %copy-start = (bf16[512,2048]{1,0:T(8,128)(2,1)S(1)}, bf16[512,2048]{1,0:T(8,128)(2,1)}, u32[]{:S(2)}) copy-start(bf16[512,2048]{1,0:T(8,128)(2,1)} %param.9) | copy-start | bytes 6291460
  5.8 16.7 %collective-permute-start.4 = (bf16[2,4,4,128]{3,2,1,0:T(4,128)(2,1)S(1)}, bf16[2,4,4,128]{3,2,1,0:T(4,128)(2,1)S(1)}, u32[]{:S(2)}, u32[]{:S(2)}) collective-permute-start(bf16[2,4,4,128]{3,2,1,0:T(4,128)(2,1)S(1)} %pad_maximum_fusion.5), channel_id=1, source_target_pairs={{0,8},{8,0},{16,24},{24,16},{32,40},{40,32},{48,56},{56,48},{4,12}... | collective-permute-start | bytes 24584 | tf_op jit(solution)/shard_map/ppermute | solution.py:20
  7.7 18.6 %collective-permute-start.5 = (bf16[2,4,4,128]{3,2,1,0:T(4,128)(2,1)S(1)}, bf16[2,4,4,128]{3,2,1,0:T(4,128)(2,1)S(1)}, u32[]{:S(2)}, u32[]{:S(2)}) collective-permute-start(bf16[2,4,4,128]{3,2,1,0:T(4,128)(2,1)S(1)} %pad_maximum_fusion.5), channel_id=1, source_target_pairs={{0,16},{8,24},{16,0},{24,8},{32,48},{40,56},{48,32},{56,40},{4,20}... | collective-permute-start | bytes 24584 | tf_op jit(solution)/shard_map/ppermute | solution.py:20
  9.3 18.5 %collective-permute-start.6 = (bf16[2,4,4,128]{3,2,1,0:T(4,128)(2,1)S(1)}, bf16[2,4,4,128]{3,2,1,0:T(4,128)(2,1)S(1)}, u32[]{:S(2)}, u32[]{:S(2)}) collective-permute-start(bf16[2,4,4,128]{3,2,1,0:T(4,128)(2,1)S(1)} %pad_maximum_fusion.5), channel_id=1, source_target_pairs={{0,24},{8,16},{16,8},{24,0},{32,56},{40,48},{48,40},{56,32},{4,28}... | collective-permute-start | bytes 24584 | tf_op jit(solution)/shard_map/ppermute | solution.py:20
  9.7 18.7 %collective-permute-start.7 = (bf16[2,4,4,128]{3,2,1,0:T(4,128)(2,1)S(1)}, bf16[2,4,4,128]{3,2,1,0:T(4,128)(2,1)S(1)}, u32[]{:S(2)}, u32[]{:S(2)}) collective-permute-start(bf16[2,4,4,128]{3,2,1,0:T(4,128)(2,1)S(1)} %pad_maximum_fusion.5), channel_id=1, source_target_pairs={{0,32},{8,40},{16,48},{24,56},{32,0},{40,8},{48,16},{56,24},{4,36}... | collective-permute-start | bytes 24584 | tf_op jit(solution)/shard_map/ppermute | solution.py:20
  15.7 19.0 %collective-permute-start.8 = (bf16[2,4,4,128]{3,2,1,0:T(4,128)(2,1)S(1)}, bf16[2,4,4,128]{3,2,1,0:T(4,128)(2,1)S(1)}, u32[]{:S(2)}, u32[]{:S(2)}) collective-permute-start(bf16[2,4,4,128]{3,2,1,0:T(4,128)(2,1)S(1)} %pad_maximum_fusion.5), channel_id=1, source_target_pairs={{0,40},{8,32},{16,56},{24,48},{32,8},{40,0},{48,24},{56,16},{4,44}... | collective-permute-start | bytes 24584 | tf_op jit(solution)/shard_map/ppermute | solution.py:20
  19.2 25.8 %copy-start.1 = (bf16[32,4,8,128]{3,2,1,0:T(8,128)(2,1)}, bf16[32,4,8,128]{3,2,1,0:T(8,128)(2,1)S(1)}, u32[]{:S(2)}) copy-start(bf16[32,4,8,128]{3,2,1,0:T(8,128)(2,1)S(1)} %fusion.28) | copy-start | bytes 786436
  22.5 13.3 %collective-permute-start.9 = (bf16[2,4,4,128]{3,2,1,0:T(4,128)(2,1)S(1)}, bf16[2,4,4,128]{3,2,1,0:T(4,128)(2,1)S(1)}, u32[]{:S(2)}, u32[]{:S(2)}) collective-permute-start(bf16[2,4,4,128]{3,2,1,0:T(4,128)(2,1)S(1)} %pad_maximum_fusion.5), channel_id=1, source_target_pairs={{0,48},{8,56},{16,32},{24,40},{32,16},{40,24},{48,0},{56,8},{4,52}... | collective-permute-start | bytes 24584 | tf_op jit(solution)/shard_map/ppermute | solution.py:20
  26.3 9.5 %collective-permute-start.10 = (bf16[2,4,4,128]{3,2,1,0:T(4,128)(2,1)S(1)}, bf16[2,4,4,128]{3,2,1,0:T(4,128)(2,1)S(1)}, u32[]{:S(2)}, u32[]{:S(2)}) collective-permute-start(bf16[2,4,4,128]{3,2,1,0:T(4,128)(2,1)S(1)} %pad_maximum_fusion.5), channel_id=1, source_target_pairs={{0,56},{8,48},{16,40},{24,32},{32,24},{40,16},{48,8},{56,0},{4,60}... | collective-permute-start | bytes 24584 | tf_op jit(solution)/shard_map/ppermute | solution.py:20
  27.8 11.4 %collective-permute-start = (bf16[2,4,32,128]{3,2,1,0:T(8,128)(2,1)S(1)}, bf16[2,4,32,128]{3,2,1,0:T(8,128)(2,1)S(1)}, u32[]{:S(2)}, u32[]{:S(2)}) collective-permute-start(bf16[2,4,32,128]{3,2,1,0:T(8,128)(2,1)S(1)} %get-tuple-element.19), channel_id=1, source_target_pairs={{240,248},{248,240},{0,8},{8,0},{244,252},{252,244},{4,12},{12,4},... | collective-permute-start | bytes 196616 | tf_op jit(solution)/shard_map/ppermute | solution.py:20
  28.4 12.2 %collective-permute-start.1 = (bf16[2,4,32,128]{3,2,1,0:T(8,128)(2,1)S(1)}, bf16[2,4,32,128]{3,2,1,0:T(8,128)(2,1)S(1)}, u32[]{:S(2)}, u32[]{:S(2)}) collective-permute-start(bf16[2,4,32,128]{3,2,1,0:T(8,128)(2,1)S(1)} %get-tuple-element.19), channel_id=1, source_target_pairs={{240,0},{248,8},{0,240},{8,248},{244,4},{252,12},{4,244},{12,252},... | collective-permute-start | bytes 196616 | tf_op jit(solution)/shard_map/ppermute | solution.py:20
  34.6 9.5 %collective-permute-start.2 = (bf16[2,4,32,128]{3,2,1,0:T(8,128)(2,1)S(1)}, bf16[2,4,32,128]{3,2,1,0:T(8,128)(2,1)S(1)}, u32[]{:S(2)}, u32[]{:S(2)}) collective-permute-start(bf16[2,4,32,128]{3,2,1,0:T(8,128)(2,1)S(1)} %get-tuple-element.19), channel_id=1, source_target_pairs={{240,8},{248,0},{0,248},{8,240},{244,12},{252,4},{4,252},{12,244},... | collective-permute-start | bytes 196616 | tf_op jit(solution)/shard_map/ppermute | solution.py:20
  35.8 9.9 %collective-permute-start.11 = (bf16[8,2,4,4,128]{4,3,2,1,0:T(4,128)(2,1)S(1)}, bf16[8,2,4,4,128]{4,3,2,1,0:T(4,128)(2,1)S(1)}, u32[]{:S(2)}, u32[]{:S(2)}) collective-permute-start(bf16[8,2,4,4,128]{4,3,2,1,0:T(4,128)(2,1)S(1)} %constant_dynamic-update-slice_fusion), channel_id=1, source_target_pairs={{0,64},{64,0},{128,192},{192,128},{4,68},{68,4},{132,196},{196,132... | collective-permute-start | bytes 196616 | tf_op jit(solution)/shard_map/ppermute | solution.py:20
  36.3 9.4 %collective-permute-start.12 = (bf16[8,2,4,4,128]{4,3,2,1,0:T(4,128)(2,1)S(1)}, bf16[8,2,4,4,128]{4,3,2,1,0:T(4,128)(2,1)}, u32[]{:S(2)}, u32[]{:S(2)}) collective-permute-start(bf16[8,2,4,4,128]{4,3,2,1,0:T(4,128)(2,1)S(1)} %constant_dynamic-update-slice_fusion), channel_id=1, source_target_pairs={{0,128},{64,192},{128,0},{192,64},{4,132},{68,196},{132,4},{196,68... | collective-permute-start | bytes 196616 | tf_op jit(solution)/shard_map/ppermute | solution.py:20
  39.2 6.5 %collective-permute-start.13 = (bf16[8,2,4,4,128]{4,3,2,1,0:T(4,128)(2,1)S(1)}, bf16[8,2,4,4,128]{4,3,2,1,0:T(4,128)(2,1)}, u32[]{:S(2)}, u32[]{:S(2)}) collective-permute-start(bf16[8,2,4,4,128]{4,3,2,1,0:T(4,128)(2,1)S(1)} %constant_dynamic-update-slice_fusion), channel_id=1, source_target_pairs={{0,192},{64,128},{128,64},{192,0},{4,196},{68,132},{132,68},{196,4... | collective-permute-start | bytes 196616 | tf_op jit(solution)/shard_map/ppermute | solution.py:20
  45.0 4.8 %collective-permute-start.3 = (bf16[4,2,4,32,128]{4,3,2,1,0:T(8,128)(2,1)}, bf16[4,2,4,32,128]{4,3,2,1,0:T(8,128)(2,1)}, u32[]{:S(2)}, u32[]{:S(2)}) collective-permute-start(bf16[4,2,4,32,128]{4,3,2,1,0:T(8,128)(2,1)} %get-tuple-element.17), channel_id=1, source_target_pairs={{0,4},{4,0},{8,12},{12,8},{16,20},{20,16},{24,28},{28,24},{32,36},... | collective-permute-start | bytes 786440 | tf_op jit(solution)/shard_map/ppermute | solution.py:20
  47.5 9.5 %collective-permute-start.14 = (bf16[4,8,2,4,4,128]{5,4,3,2,1,0:T(4,128)(2,1)}, bf16[4,8,2,4,4,128]{5,4,3,2,1,0:T(4,128)(2,1)}, u32[]{:S(2)}, u32[]{:S(2)}) collective-permute-start(bf16[4,8,2,4,4,128]{5,4,3,2,1,0:T(4,128)(2,1)} %pad_maximum_fusion.3), channel_id=1, source_target_pairs={{0,4},{4,0},{8,12},{12,8},{16,20},{20,16},{24,28},{28,24},{32,36},... | collective-permute-start | bytes 786440 | tf_op jit(solution)/shard_map/ppermute | solution.py:20
  65.0 21.4 %copy-start.7 = (f32[2048]{0:T(1024)S(1)}, f32[2048]{0:T(1024)}, u32[]{:S(2)}) copy-start(f32[2048]{0:T(1024)} %param.10) | copy-start | bytes 24580
  65.9 9.4 %collective-permute-start.15 = (bf16[64,2048]{1,0:T(8,128)(2,1)}, bf16[64,2048]{1,0:T(8,128)(2,1)S(1)}, u32[]{:S(2)}, u32[]{:S(2)}) collective-permute-start(bf16[64,2048]{1,0:T(8,128)(2,1)} %get-tuple-element.9), channel_id=1, source_target_pairs={{0,1},{1,0},{2,3},{3,2},{4,5},{5,4},{6,7},{7,6},{8,9},{9,8},{10,11... | collective-permute-start | bytes 786440 | tf_op jit(solution)/shard_map/ppermute | solution.py:111
  67.4 14.9 %collective-permute-start.16 = (bf16[64,2048]{1,0:T(8,128)(2,1)}, bf16[64,2048]{1,0:T(8,128)(2,1)}, u32[]{:S(2)}, u32[]{:S(2)}) collective-permute-start(bf16[64,2048]{1,0:T(8,128)(2,1)} %get-tuple-element.11), channel_id=1, source_target_pairs={{0,2},{1,3},{2,0},{3,1},{4,6},{5,7},{6,4},{7,5},{8,10},{9,11},{10,... | collective-permute-start | bytes 786440 | tf_op jit(solution)/shard_map/ppermute | solution.py:111
  70.1 14.8 %collective-permute-start.17 = (bf16[64,2048]{1,0:T(8,128)(2,1)}, bf16[64,2048]{1,0:T(8,128)(2,1)}, u32[]{:S(2)}, u32[]{:S(2)}) collective-permute-start(bf16[64,2048]{1,0:T(8,128)(2,1)} %get-tuple-element.10), channel_id=1, source_target_pairs={{0,3},{1,2},{2,1},{3,0},{4,7},{5,6},{6,5},{7,4},{8,11},{9,10},{10,... | collective-permute-start | bytes 786440 | tf_op jit(solution)/shard_map/ppermute | solution.py:111
  88.6 4.7 %collective-permute-start.18 = (f32[64,128]{1,0:T(8,128)}, f32[64,128]{1,0:T(8,128)S(1)}, u32[]{:S(2)}, u32[]{:S(2)}) collective-permute-start(f32[64,128]{1,0:T(8,128)} %get-tuple-element.27), channel_id=1, source_target_pairs={{0,1},{1,0},{2,3},{3,2},{4,5},{5,4},{6,7},{7,6},{8,9},{9,8},{10,11... | collective-permute-start | bytes 98312 | tf_op jit(solution)/shard_map/ppermute | solution.py:20
  88.6 5.6 %collective-permute-start.19 = (f32[64,128]{1,0:T(8,128)}, f32[64,128]{1,0:T(8,128)S(1)}, u32[]{:S(2)}, u32[]{:S(2)}) collective-permute-start(f32[64,128]{1,0:T(8,128)} %get-tuple-element.27), channel_id=1, source_target_pairs={{0,2},{1,3},{2,0},{3,1},{4,6},{5,7},{6,4},{7,5},{8,10},{9,11},{10,... | collective-permute-start | bytes 98312 | tf_op jit(solution)/shard_map/ppermute | solution.py:20
  90.5 5.3 %collective-permute-start.20 = (f32[64,128]{1,0:T(8,128)}, f32[64,128]{1,0:T(8,128)S(1)}, u32[]{:S(2)}, u32[]{:S(2)}) collective-permute-start(f32[64,128]{1,0:T(8,128)} %get-tuple-element.27), channel_id=1, source_target_pairs={{0,3},{1,2},{2,1},{3,0},{4,7},{5,6},{6,5},{7,4},{8,11},{9,10},{10,... | collective-permute-start | bytes 98312 | tf_op jit(solution)/shard_map/ppermute | solution.py:20
  (11 other events, 69.4 us)

commit v2 on v1

v2 whole, which is shorter than its diff:
```python
import functools

import jax
import jax.numpy as jnp
from jax import lax
from jax.experimental import pallas as pl
from jax.experimental.pallas import tpu as pltpu
from jax.sharding import PartitionSpec as P

SPAN = 8
PICKS = 40
LOW = -1e30
VMEM = pl.BlockSpec(memory_space=pltpu.VMEM)
SMEM = pl.BlockSpec(memory_space=pltpu.SMEM)
PARAMS = pltpu.CompilerParams(vmem_limit_bytes=48 << 20)


def segments(seq_count):
    return [
        [(SPAN * k - SPAN // 2 + i) % seq_count for i in range(SPAN)]
        for k in range(seq_count // SPAN)
    ]


def share(block, axis, groups):
    pieces = [block]
    for step in range(1, len(groups[0])):
        route = [(g[i], g[i ^ step]) for g in groups for i in range(len(g))]
        pieces.append(lax.ppermute(block, axis, route))
    return pieces


def dot(a, b):
    return jnp.dot(a, b, preferred_element_type=jnp.float32)


def dot_t(a, b):
    return lax.dot_general(a, b, (((1,), (1,)), ((), ())), preferred_element_type=jnp.float32)


def picked_rows(c, mid, far, mid_rows, seq_count):
    last = (c >= mid_rows) & (c < mid_rows + 4)
    other = jnp.where(last, (c - mid_rows) * seq_count + far, -1)
    return jnp.where(c < mid_rows, c * SPAN + mid, other)


def kv_kernel(rows, heads, size, seq_count, mid_ref, far_ref, tok_ref, w_ref,
              kv_ref, mid_out, far_out, acc_ref, few_ref):
    step = pl.program_id(1)
    part = dot(tok_ref[...], w_ref[...])

    @pl.when(step == 0)
    def _():
        acc_ref[...] = part

    @pl.when(step > 0)
    def _():
        acc_ref[...] += part

    @pl.when(step == pl.num_programs(1) - 1)
    def _():
        whole = acc_ref[...].astype(jnp.bfloat16)
        kv_ref[...] = whole
        mid_rows = rows // SPAN
        c = lax.broadcasted_iota(jnp.int32, (PICKS, rows), 0)
        r = lax.broadcasted_iota(jnp.int32, (PICKS, rows), 1)
        for h in range(heads):
            target = picked_rows(c, mid_ref[h], far_ref[h], mid_rows, seq_count)
            marks = jnp.where(r == target, 1.0, 0.0).astype(jnp.bfloat16)
            got = dot(marks, whole[:, h * size : (h + 1) * size])
            mid_out[h] = got[:mid_rows].astype(jnp.bfloat16)
            few_ref[pl.ds(4 * h, 4)] = got[mid_rows : mid_rows + 4]
        far_out[...] = few_ref[...].astype(jnp.bfloat16)


def near_kernel(rows, heads, size, seq_count, mid_ref, far_ref, tok_ref, w_ref, kv_ref,
                near_ref, sel_ref, acc_ref):
    step = pl.program_id(0)
    part = dot(tok_ref[...], w_ref[...])

    @pl.when(step == 0)
    def _():
        acc_ref[...] = part

    @pl.when(step > 0)
    def _():
        acc_ref[...] += part

    @pl.when(step == pl.num_programs(0) - 1)
    def _():
        whole = acc_ref[...].astype(jnp.bfloat16)
        mid_rows = rows // SPAN
        c = lax.broadcasted_iota(jnp.int32, (PICKS, rows), 0)
        r = lax.broadcasted_iota(jnp.int32, (PICKS, rows), 1)
        for h in range(heads):
            cols = slice(h * size, (h + 1) * size)
            queries = whole[:, cols]
            target = picked_rows(c, mid_ref[h], far_ref[h], mid_rows, seq_count)
            marks = jnp.where(r == target, 1.0, 0.0).astype(jnp.bfloat16)
            sel_ref[h] = dot(marks, queries).astype(jnp.bfloat16)
            scores = dot_t(queries, kv_ref[0, :, cols]) * size**-0.5
            top = jnp.max(scores, axis=1, keepdims=True)
            weights = jnp.exp(scores - top)
            total = jnp.sum(weights, axis=1, keepdims=True)
            summed = dot(weights.astype(jnp.bfloat16), kv_ref[1, :, cols])
            near_ref[:, cols] = (summed / total).astype(jnp.bfloat16)


def softmax_parts(scores, values):
    top = jnp.max(scores, axis=1, keepdims=True)
    weights = jnp.exp(scores - top)
    total = jnp.sum(weights, axis=1, keepdims=True)
    return top, total, dot(weights.astype(jnp.bfloat16), values)


def wide_kernel(rows, heads, size, seq_count, quarters,
                mid_ref, far_ref, place_ref, sel_ref, kv_ref, near_ref, *refs):
    mid_pieces, mid_other, far_pieces, far_other, w_ref = (
        refs[0:4], refs[4], refs[5:9], refs[9], refs[10]
    )
    outs, attn_ref = refs[11 : 11 + quarters], refs[11 + quarters]
    mid_rows = rows // SPAN
    scale = size**-0.5
    far_rows = lambda i: jnp.concatenate(
        [ref[:, i].reshape(-1, size) for ref in far_pieces]
        + [far_other[j, :, i].reshape(-1, size) for j in range(4)]
    )
    far_q = jnp.concatenate([sel_ref[h].astype(jnp.float32)[mid_rows:] for h in range(heads)])
    far_scores = dot_t(far_q.astype(jnp.bfloat16), far_rows(0)) * scale
    q_head = lax.broadcasted_iota(jnp.int32, far_scores.shape, 0) // 8
    k_head = (lax.broadcasted_iota(jnp.int32, far_scores.shape, 1) % 16) // 4
    far_top, far_total, far_sum = softmax_parts(
        jnp.where(q_head == k_head, far_scores, LOW), far_rows(1)
    )
    for h in range(heads):
        cols = slice(h * size, (h + 1) * size)
        mid_off, far_off = mid_ref[h], far_ref[h]
        stack = lambda i: jnp.concatenate(
            [kv_ref[i, :, cols]]
            + [ref[i, h] for ref in mid_pieces]
            + [mid_other[j, i, h] for j in range(4)]
        )
        scores = dot_t(sel_ref[h], stack(0)) * scale
        row = lax.broadcasted_iota(jnp.int32, scores.shape, 0)
        col = lax.broadcasted_iota(jnp.int32, scores.shape, 1)
        both = ((far_off + SPAN - mid_off) & (SPAN - 1)) == 0
        keep = (row < mid_rows) | (col < rows) | both
        top, total, summed = softmax_parts(jnp.where(keep, scores, LOW), stack(1))
        attn = summed / total
        far = slice(8 * h, 8 * h + 8)
        peak = jnp.maximum(top[mid_rows:], far_top[far])
        mine = jnp.exp(top[mid_rows:] - peak)
        other = jnp.exp(far_top[far] - peak)
        attn_far = (mine * summed[mid_rows:] + other * far_sum[far]) / (
            mine * total[mid_rows:] + other * far_total[far]
        )
        attn = jnp.concatenate([attn[:mid_rows], attn_far]).astype(jnp.bfloat16)
        r = lax.broadcasted_iota(jnp.int32, (rows, PICKS), 0)
        c = lax.broadcasted_iota(jnp.int32, (rows, PICKS), 1)
        target = picked_rows(c, mid_off, far_off, mid_rows, seq_count)
        twice = (c < mid_rows) & (
            ((target + seq_count - far_off) & (seq_count - 1)) == 0
        )
        marks = jnp.where((r == target) & jnp.logical_not(twice), 1.0, 0.0)
        hit = jnp.sum(marks, axis=1, keepdims=True) > 0.5
        put = dot(marks.astype(jnp.bfloat16), attn)
        attn_ref[:, cols] = jnp.where(hit, put, near_ref[:, cols].astype(jnp.float32))
    own = rows // quarters
    place = place_ref[0]
    order = jnp.concatenate(
        [
            attn_ref[pl.ds(pl.multiple_of((place ^ s) * own, own), own), :]
            for s in range(quarters)
        ]
    ).astype(jnp.bfloat16)
    chunk = 512
    for start in range(0, w_ref.shape[1], chunk):
        part = dot(order, w_ref[:, start : start + chunk]).astype(jnp.bfloat16)
        for s in range(quarters):
            outs[s][:, start : start + chunk] = part[s * own : (s + 1) * own]


def logits_kernel(place_ref, tok_ref, gain_ref, label_ref, *refs):
    out_ref = refs[-1]
    mixed = tok_ref[...].astype(jnp.float32)
    for ref in refs[:-1]:
        mixed = mixed + ref[...].astype(jnp.float32)
    mean_sq = jnp.mean(mixed * mixed, axis=1, keepdims=True)
    scaled = (mixed * gain_ref[...]).astype(jnp.bfloat16)
    out_ref[...] = dot(scaled, label_ref[...]) / jnp.sqrt(mean_sq + 1e-05)


def body(tokens, w_qkv, w_out, norm_gain, w_label, offset_mid, offset_far):
    rows, width = tokens.shape
    heads = offset_mid.shape[0]
    cols = w_qkv.shape[2]
    size = cols // heads
    seq_count = lax.axis_size("seq")
    head_count = lax.axis_size("head")
    place = lax.axis_index("head")
    mid_rows = rows // SPAN
    sizes = (rows, heads, size, seq_count)
    bf16 = lambda *shape: jax.ShapeDtypeStruct(shape, jnp.bfloat16)
    weights = w_qkv.transpose(1, 0, 2)
    deep = 512

    kv, mid_kv, far_kv = pl.pallas_call(
        functools.partial(kv_kernel, *sizes),
        grid=(2, width // deep),
        in_specs=[
            SMEM,
            SMEM,
            pl.BlockSpec((rows, deep), lambda c, k: (0, k)),
            pl.BlockSpec((None, deep, cols), lambda c, k: (1 + c, k, 0)),
        ],
        out_specs=[
            pl.BlockSpec((None, rows, cols), lambda c, k: (c, 0, 0)),
            pl.BlockSpec((None, heads, mid_rows, size), lambda c, k: (c, 0, 0, 0)),
            pl.BlockSpec((None, 4 * heads, size), lambda c, k: (c, 0, 0)),
        ],
        out_shape=[bf16(2, rows, cols), bf16(2, heads, mid_rows, size), bf16(2, 4 * heads, size)],
        scratch_shapes=[
            pltpu.VMEM((rows, cols), jnp.float32),
            pltpu.VMEM((4 * heads, size), jnp.float32),
        ],
        compiler_params=PARAMS,
        name="keys_values",
    )(offset_mid, offset_far, tokens, weights)

    groups = segments(seq_count)
    across = [[g[2 * i + c] for i in range(SPAN // 2)] for g in groups for c in range(2)]
    cores = [(i, i ^ 1) for i in range(seq_count)]
    along_z = [[16 * y + 2 * z + c for z in range(8)] for y in range(4) for c in range(2)]
    along_y = [[16 * y + r for y in range(4)] for r in range(16)]
    mid_pieces = share(mid_kv, "seq", across)
    mid_other = lax.ppermute(jnp.stack(mid_pieces), "seq", cores)
    far_line = lax.all_to_all(
        jnp.broadcast_to(far_kv[None], (8,) + far_kv.shape), "seq", 0, 0, axis_index_groups=along_z
    )
    far_pieces = share(far_line, "seq", along_y)
    far_other = lax.ppermute(jnp.stack(far_pieces), "seq", cores)

    near, sel = pl.pallas_call(
        functools.partial(near_kernel, *sizes),
        grid=(width // deep,),
        in_specs=[
            SMEM,
            SMEM,
            pl.BlockSpec((rows, deep), lambda k: (0, k)),
            pl.BlockSpec((None, deep, cols), lambda k: (0, k, 0)),
            pl.BlockSpec((2, rows, cols), lambda k: (0, 0, 0)),
        ],
        out_specs=[
            pl.BlockSpec((rows, cols), lambda k: (0, 0)),
            pl.BlockSpec((heads, PICKS, size), lambda k: (0, 0, 0)),
        ],
        out_shape=[bf16(rows, cols), bf16(heads, PICKS, size)],
        scratch_shapes=[pltpu.VMEM((rows, cols), jnp.float32)],
        compiler_params=PARAMS,
        name="near",
    )(offset_mid, offset_far, tokens, weights, kv)

    own = rows // head_count
    place_arr = place.astype(jnp.int32).reshape(1)
    parts = pl.pallas_call(
        functools.partial(wide_kernel, *sizes, head_count),
        in_specs=[SMEM] * 3 + [VMEM] * 14,
        out_specs=[VMEM] * head_count,
        out_shape=[bf16(own, width)] * head_count,
        scratch_shapes=[pltpu.VMEM((rows, cols), jnp.float32)],
        compiler_params=PARAMS,
        name="wide",
    )(
        offset_mid, offset_far, place_arr, sel, kv, near,
        *mid_pieces, mid_other, *far_pieces, far_other, w_out,
    )

    got = [parts[0]]
    for step in range(1, head_count):
        route = [(i, i ^ step) for i in range(head_count)]
        got.append(lax.ppermute(parts[step], "head", route))

    whole = lambda *shape: pl.BlockSpec(shape, lambda i, p: (0,) * len(shape))
    logit = pl.pallas_call(
        logits_kernel,
        grid_spec=pltpu.PrefetchScalarGridSpec(
            num_scalar_prefetch=1,
            grid=(1,),
            in_specs=[
                pl.BlockSpec((own, width), lambda i, p: (p[0], 0)),
                whole(1, width),
                whole(*w_label.shape),
            ]
            + [whole(own, width)] * head_count,
            out_specs=whole(own, w_label.shape[1]),
        ),
        out_shape=jax.ShapeDtypeStruct((own, w_label.shape[1]), jnp.float32),
        compiler_params=PARAMS,
        name="logits",
    )(place_arr, tokens, norm_gain.reshape(1, width), w_label, *got)

    every = share(logit, "head", [list(range(head_count))])
    logits = jnp.zeros((head_count,) + logit.shape, jnp.float32)
    for step in range(head_count):
        logits = lax.dynamic_update_index_in_dim(logits, every[step], place ^ step, 0)
    return logits.reshape(rows, -1)


def solution(mesh):
    return jax.shard_map(
        body,
        mesh=mesh,
        in_specs=(
            P("seq", None),
            P(None, None, "head"),
            P("head", None),
            P(),
            P(),
            P("head"),
            P("head"),
        ),
        out_specs=P("seq", None),
        check_vma=False,
    )
```

time: 97 us -> 73 us (0.75)
  matrix products: 21.9 us -> 0 us
  Pallas kernels: 0 us -> 15.6 us
  other arithmetic: 11.1 us -> 0.79 us
  starting transfers between devices: 38.7 us -> 31 us
    dot_general x21 -> x0, matrix products: 21.9 us -> none  [the longest x3 7.69 us: body(): jnp.dot(tokens, w_qkv[:, c], preferred_element_type=jnp.float32)]
    ppermute x18 -> x9, starting transfers between devices: 34 us -> 17.2 us  [share(): pieces.append(lax.ppermute(block, axis, route))]
    pallas_call x0 -> x4, Pallas kernels: none -> 15.6 us  [the longest x1 6.69 us: body(): pl.pallas_call(functools.partial(kv_kernel, *sizes), grid=(2, width // de...]
    all_to_all x0 -> x1, starting transfers between devices: none -> 8.57 us  [body(): lax.all_to_all(jnp.broadcast_to(far_kv[None], (8,) + far_kv.shape), 'seq'...]
    another operation x7 -> x2, other arithmetic: 7.03 us -> 0.79 us  [the longest x1 0.75 us: body(): far_other = lax.ppermute(jnp.stack(far_pieces), 'seq', cores)]
    ppermute x18 -> x9, waiting for transfers between devices: 6.11 us -> 8.71 us  [share(): pieces.append(lax.ppermute(block, axis, route))]
    ppermute x3 -> x5, waiting for transfers between devices: 14.3 us -> 11.8 us  [the longest x3 11.8 us: body(): got.append(lax.ppermute(parts[step], 'head', route))]
    reduce_sum x4 -> x0, other arithmetic: 2.5 us -> none  [the longest x1 1.4 us: body(): mean_sq = jnp.mean(mixed * mixed, axis=-1)]
  transfers between devices with their start and end apart: 21 -> 15, of which waited for: 6 -> 6; matrix products, arithmetic and copies ran while one was open for 19% -> 1% of each run, Pallas kernels for 0% -> 6%
where the time goes in v2:
time: 73 us; the launch traced here: 72 us
  starting transfers between devices  31 us (42%)
  waiting for transfers between devices  20.5 us (28%)
  Pallas kernels  15.6 us (21%)
  local copies, waits for them, and re-layouts  3.92 us (5%)
  other arithmetic  0.79 us (1%)
    ppermute x9, starting transfers between devices, share(): pieces.append(lax.ppermute(block, axis, route))  17.2 us
    ppermute x3, waiting for transfers between devices, body(): got.append(lax.ppermute(parts[step], 'head', route))  11.8 us
    ppermute x9, waiting for transfers between devices, share(): pieces.append(lax.ppermute(block, axis, route))  8.71 us
    all_to_all x1, starting transfers between devices, body(): lax.all_to_all(jnp.broadcast_to(far_kv[None], (8,) + far_kv.shape), 'seq'...  8.57 us
    pallas_call x1, Pallas kernels, body(): pl.pallas_call(functools.partial(kv_kernel, *sizes), grid=(2, width // de...  6.69 us
    ppermute x3, starting transfers between devices, body(): got.append(lax.ppermute(parts[step], 'head', route))  4.7 us
    pallas_call x1, Pallas kernels, body(): pl.pallas_call(functools.partial(near_kernel, *sizes), grid=(width // dee...  4.49 us
    pallas_call x1, Pallas kernels, body(): pl.pallas_call(functools.partial(wide_kernel, *sizes, head_count), in_spe...  4.1 us
  transfers between devices with their start and end apart: 15, of which 6 were waited for; matrix products, arithmetic and copies ran while one was open for 1% of the time, Pallas kernels for 6%

profile of v2, /device:TPU:32, one launch (start us, length us, event | category | flops | bytes accessed | tf_op | source)
XLA Modules:
  0.0 72.0 jit_solution(6916261081821995322)
XLA Ops:
  0.0 1.2 %copy-done = bf16[256,2048]{1,0:T(8,128)(2,1)S(1)} copy-done((bf16[256,2048]{1,0:T(8,128)(2,1)S(1)}, bf16[256,2048]{1,0:T(8,128)(2,1)}, u32[]{:S(2)}) %copy-start) | copy-done | bytes 1048600
  1.3 0.7 copy-done.5
  1.9 0.7 copy-done.7
  2.6 6.7 %keys_values.1 = (bf16[2,256,512]{2,1,0:T(8,128)(2,1)S(1)}, bf16[2,4,32,128]{3,2,1,0:T(8,128)(2,1)S(1)}, bf16[2,16,128]{2,1,0:T(8,128)(2,1)S(1)}) custom-call(s32[4]{0:T(128)S(1)} %copy-done.5, s32[4]{0:T(128)S(1)} %copy-done.7, bf16[256,2048]{1,0:T(8,128)(2,1)S(1)} %copy-done, bf16[3,2048,512]{2,1,0:T(8,128)(2,1)} %bitcast.29), custom_call_target="tpu_custom_call" | custom-call | tf_op jit(solution)/shard_map/keys_values/pallas_call | solution.py:207
  9.3 0.6 broadcast_in_dim.23
  9.9 8.6 %all-to-all-start = ((bf16[8,2,16,128]{3,2,1,0:T(8,128)(2,1)}), bf16[8,2,16,128]{3,2,1,0:T(8,128)(2,1)S(1)}, u32[]{:S(2)}, u32[]{:S(2)}) async-start(bf16[8,2,16,128]{3,2,1,0:T(8,128)(2,1)} %broadcast_in_dim.23), calls=%async_computation | async-start | bytes 131072 | tf_op jit(solution)/shard_map/all_to_all | solution.py:237
  18.5 6.6 %collective-permute-start.1 = (bf16[2,4,32,128]{3,2,1,0:T(8,128)(2,1)S(1)}, bf16[2,4,32,128]{3,2,1,0:T(8,128)(2,1)S(1)}, u32[]{:S(2)}, u32[]{:S(2)}) collective-permute-start(bf16[2,4,32,128]{3,2,1,0:T(8,128)(2,1)S(1)} %get-tuple-element.17.refs_0_), channel_id=1, source_target_pairs={{240,0},{248,8},{0,240},{8,248},{244,4},{252,12},{4,244},{12,252},... | collective-permute-start | bytes 196616 | tf_op jit(solution)/shard_map/ppermute | solution.py:29
  25.1 1.1 %collective-permute-start.2 = (bf16[2,4,32,128]{3,2,1,0:T(8,128)(2,1)S(1)}, bf16[2,4,32,128]{3,2,1,0:T(8,128)(2,1)S(1)}, u32[]{:S(2)}, u32[]{:S(2)}) collective-permute-start(bf16[2,4,32,128]{3,2,1,0:T(8,128)(2,1)S(1)} %get-tuple-element.17.refs_0_), channel_id=1, source_target_pairs={{240,8},{248,0},{0,248},{8,240},{244,12},{252,4},{4,252},{12,244},... | collective-permute-start | bytes 196616 | tf_op jit(solution)/shard_map/ppermute | solution.py:29
  26.2 2.5 %collective-permute-start.6 = (bf16[8,2,16,128]{3,2,1,0:T(8,128)(2,1)S(1)}, bf16[8,2,16,128]{3,2,1,0:T(8,128)(2,1)S(1)}, u32[]{:S(2)}, u32[]{:S(2)}) collective-permute-start(bf16[8,2,16,128]{3,2,1,0:T(8,128)(2,1)S(1)} %all-to-all-done.refs_5_), channel_id=1, source_target_pairs={{0,192},{64,128},{128,64},{192,0},{4,196},{68,132},{132,68},{196,4... | collective-permute-start | bytes 196616 | tf_op jit(solution)/shard_map/ppermute | solution.py:29
  28.8 2.1 %collective-permute-start.5 = (bf16[8,2,16,128]{3,2,1,0:T(8,128)(2,1)S(1)}, bf16[8,2,16,128]{3,2,1,0:T(8,128)(2,1)S(1)}, u32[]{:S(2)}, u32[]{:S(2)}) collective-permute-start(bf16[8,2,16,128]{3,2,1,0:T(8,128)(2,1)S(1)} %all-to-all-done.refs_5_), channel_id=1, source_target_pairs={{0,128},{64,192},{128,0},{192,64},{4,132},{68,196},{132,4},{196,68... | collective-permute-start | bytes 196616 | tf_op jit(solution)/shard_map/ppermute | solution.py:29
  30.9 4.1 %collective-permute-done.2.refs_3_ = bf16[2,4,32,128]{3,2,1,0:T(8,128)(2,1)S(1)} collective-permute-done((bf16[2,4,32,128]{3,2,1,0:T(8,128)(2,1)S(1)}, bf16[2,4,32,128]{3,2,1,0:T(8,128)(2,1)S(1)}, u32[]{:S(2)}, u32[]{:S(2)}) %collective-permute-start.2) | collective-permute-done | bytes 65568 | tf_op jit(solution)/shard_map/ppermute | solution.py:29
  35.2 0.8 %pad_maximum_fusion.1 = bf16[4,8,2,16,128]{4,3,2,1,0:T(8,128)(2,1)} fusion(bf16[1,8,2,16,128]{4,3,2,1,0:T(8,128)(2,1)S(1)} %bitcast.25, bf16[1,8,2,16,128]{4,3,2,1,0:T(8,128)(2,1)S(1)} %bitcast.27, bf16[1,8,2,16,128]{4,3,2,1,0:T(8,128)(2,1)S(1)} %bitcast.26, bf16[1,8,2,16,128]{4,3,2,1,0:T(8,128)(2,1)S(1)} %bitcast.20), kind=kLoop, calls=%fused_computation.1 | loop fusion | flops 393216 | bytes 524288 | tf_op jit(solution)/shard_map/stack | solution.py:241
  36.0 0.5 collective-permute-start.7
  36.4 4.5 %near.1 = (bf16[256,512]{1,0:T(8,128)(2,1)S(1)}, bf16[4,40,128]{2,1,0:T(8,128)(2,1)S(1)}) custom-call(s32[4]{0:T(128)S(1)} %copy-done.6, s32[4]{0:T(128)S(1)} %copy-done.8, bf16[256,2048]{1,0:T(8,128)(2,1)S(1)} %copy-done.1, bf16[3,2048,512]{2,1,0:T(8,128)(2,1)} %bitcast.30, bf16[2,256,512]{2,1,0:T(8,128)(2,1)S(1)} %get-tuple-element.14.kv_ref), custom_call_target="tpu_custom_call" | custom-call | tf_op jit(solution)/shard_map/near/pallas_call | solution.py:243
  41.0 4.1 %wide.1 = (bf16[64,2048]{1,0:T(8,128)(2,1)S(1)}, bf16[64,2048]{1,0:T(8,128)(2,1)}, bf16[64,2048]{1,0:T(8,128)(2,1)}, bf16[64,2048]{1,0:T(8,128)(2,1)}) custom-call(s32[4]{0:T(128)S(1)} %copy-done.6, s32[4]{0:T(128)S(1)} %copy-done.8, s32[1]{0:T(128)} %bitcast.place_ref, bf16[4,40,128]{2,1,0:T(8,128)(2,1)S(1)} %get-tuple-element.15.sel_ref, ...), custom_call_target="tpu_custom_call" | custom-call | tf_op jit(solution)/shard_map/wide/pallas_call | solution.py:265
  45.1 2.8 %collective-permute-start.10 = (bf16[64,2048]{1,0:T(8,128)(2,1)}, bf16[64,2048]{1,0:T(8,128)(2,1)S(1)}, u32[]{:S(2)}, u32[]{:S(2)}) collective-permute-start(bf16[64,2048]{1,0:T(8,128)(2,1)} %get-tuple-element.22), channel_id=1, source_target_pairs={{0,3},{1,2},{2,1},{3,0},{4,7},{5,6},{6,5},{7,4},{8,11},{9,10},{10,... | collective-permute-start | bytes 786440 | tf_op jit(solution)/shard_map/ppermute | solution.py:281
  48.1 1.7 %collective-permute-start.9 = (bf16[64,2048]{1,0:T(8,128)(2,1)}, bf16[64,2048]{1,0:T(8,128)(2,1)S(1)}, u32[]{:S(2)}, u32[]{:S(2)}) collective-permute-start(bf16[64,2048]{1,0:T(8,128)(2,1)} %get-tuple-element.21), channel_id=1, source_target_pairs={{0,2},{1,3},{2,0},{3,1},{4,6},{5,7},{6,4},{7,5},{8,10},{9,11},{10,... | collective-permute-start | bytes 786440 | tf_op jit(solution)/shard_map/ppermute | solution.py:281
  49.8 5.0 %collective-permute-done.10.refs_3_ = bf16[64,2048]{1,0:T(8,128)(2,1)S(1)} collective-permute-done((bf16[64,2048]{1,0:T(8,128)(2,1)}, bf16[64,2048]{1,0:T(8,128)(2,1)S(1)}, u32[]{:S(2)}, u32[]{:S(2)}) %collective-permute-start.10) | collective-permute-done | bytes 262176 | tf_op jit(solution)/shard_map/ppermute | solution.py:281
  54.8 2.5 %collective-permute-done.8.refs_1_ = bf16[64,2048]{1,0:T(8,128)(2,1)S(1)} collective-permute-done((bf16[64,2048]{1,0:T(8,128)(2,1)}, bf16[64,2048]{1,0:T(8,128)(2,1)S(1)}, u32[]{:S(2)}, u32[]{:S(2)}) %collective-permute-start.8) | collective-permute-done | bytes 262176 | tf_op jit(solution)/shard_map/ppermute | solution.py:281
  57.2 4.3 %collective-permute-done.9.refs_2_ = bf16[64,2048]{1,0:T(8,128)(2,1)S(1)} collective-permute-done((bf16[64,2048]{1,0:T(8,128)(2,1)}, bf16[64,2048]{1,0:T(8,128)(2,1)S(1)}, u32[]{:S(2)}, u32[]{:S(2)}) %collective-permute-start.9) | collective-permute-done | bytes 262176 | tf_op jit(solution)/shard_map/ppermute | solution.py:281
  62.2 3.9 %collective-permute-start.12 = (f32[64,128]{1,0:T(8,128)S(1)}, f32[64,128]{1,0:T(8,128)S(1)}, u32[]{:S(2)}, u32[]{:S(2)}) collective-permute-start(f32[64,128]{1,0:T(8,128)S(1)} %logits.1), channel_id=1, source_target_pairs={{0,2},{1,3},{2,0},{3,1},{4,6},{5,7},{6,4},{7,5},{8,10},{9,11},{10,... | collective-permute-start | bytes 98312 | tf_op jit(solution)/shard_map/ppermute | solution.py:29
  66.7 1.7 %collective-permute-done.12 = f32[64,128]{1,0:T(8,128)S(1)} collective-permute-done((f32[64,128]{1,0:T(8,128)S(1)}, f32[64,128]{1,0:T(8,128)S(1)}, u32[]{:S(2)}, u32[]{:S(2)}) %collective-permute-start.12) | collective-permute-done | bytes 32800 | tf_op jit(solution)/shard_map/ppermute | solution.py:29
  68.4 2.9 %collective-permute-done.13 = f32[64,128]{1,0:T(8,128)S(1)} collective-permute-done((f32[64,128]{1,0:T(8,128)S(1)}, f32[64,128]{1,0:T(8,128)S(1)}, u32[]{:S(2)}, u32[]{:S(2)}) %collective-permute-start.13) | collective-permute-done | bytes 32800 | tf_op jit(solution)/shard_map/ppermute | solution.py:29
  71.3 0.7 copy-done.9
  (38 shorter events, 1.8 us)
Async XLA Ops:
  0.0 36.4 %copy-start.6 = (s32[4]{0:T(128)S(1)}, s32[4]{0:T(128)}, u32[]{:S(2)}) copy-start(s32[4]{0:T(128)} %mid_ref.5) | copy-start | bytes 52
  0.0 36.4 %copy-start.8 = (s32[4]{0:T(128)S(1)}, s32[4]{0:T(128)}, u32[]{:S(2)}) copy-start(s32[4]{0:T(128)} %far_ref.5) | copy-start | bytes 52
  0.0 1.3 %copy-start = (bf16[256,2048]{1,0:T(8,128)(2,1)S(1)}, bf16[256,2048]{1,0:T(8,128)(2,1)}, u32[]{:S(2)}) copy-start(bf16[256,2048]{1,0:T(8,128)(2,1)} %tok_ref.5) | copy-start | bytes 3145732
  1.3 0.7 copy-start.5
  1.9 0.7 copy-start.7
  2.6 33.9 %copy-start.1 = (bf16[256,2048]{1,0:T(8,128)(2,1)S(1)}, bf16[256,2048]{1,0:T(8,128)(2,1)}, u32[]{:S(2)}) copy-start(bf16[256,2048]{1,0:T(8,128)(2,1)} %tok_ref.5) | copy-start | bytes 3145732
  9.9 16.3 %all-to-all-start = ((bf16[8,2,16,128]{3,2,1,0:T(8,128)(2,1)}), bf16[8,2,16,128]{3,2,1,0:T(8,128)(2,1)S(1)}, u32[]{:S(2)}, u32[]{:S(2)}) async-start(bf16[8,2,16,128]{3,2,1,0:T(8,128)(2,1)} %broadcast_in_dim.23), calls=%async_computation | async-start | bytes 131072 | tf_op jit(solution)/shard_map/all_to_all | solution.py:237
  18.5 10.3 %collective-permute-start = (bf16[2,4,32,128]{3,2,1,0:T(8,128)(2,1)S(1)}, bf16[2,4,32,128]{3,2,1,0:T(8,128)(2,1)S(1)}, u32[]{:S(2)}, u32[]{:S(2)}) collective-permute-start(bf16[2,4,32,128]{3,2,1,0:T(8,128)(2,1)S(1)} %get-tuple-element.17.refs_0_), channel_id=1, source_target_pairs={{240,248},{248,240},{0,8},{8,0},{244,252},{252,244},{4,12},{12,4},... | collective-permute-start | bytes 196616 | tf_op jit(solution)/shard_map/ppermute | solution.py:29
  18.5 12.4 %collective-permute-start.1 = (bf16[2,4,32,128]{3,2,1,0:T(8,128)(2,1)S(1)}, bf16[2,4,32,128]{3,2,1,0:T(8,128)(2,1)S(1)}, u32[]{:S(2)}, u32[]{:S(2)}) collective-permute-start(bf16[2,4,32,128]{3,2,1,0:T(8,128)(2,1)S(1)} %get-tuple-element.17.refs_0_), channel_id=1, source_target_pairs={{240,0},{248,8},{0,240},{8,248},{244,4},{252,12},{4,244},{12,252},... | collective-permute-start | bytes 196616 | tf_op jit(solution)/shard_map/ppermute | solution.py:29
  25.1 9.9 %collective-permute-start.2 = (bf16[2,4,32,128]{3,2,1,0:T(8,128)(2,1)S(1)}, bf16[2,4,32,128]{3,2,1,0:T(8,128)(2,1)S(1)}, u32[]{:S(2)}, u32[]{:S(2)}) collective-permute-start(bf16[2,4,32,128]{3,2,1,0:T(8,128)(2,1)S(1)} %get-tuple-element.17.refs_0_), channel_id=1, source_target_pairs={{240,8},{248,0},{0,248},{8,240},{244,12},{252,4},{4,252},{12,244},... | collective-permute-start | bytes 196616 | tf_op jit(solution)/shard_map/ppermute | solution.py:29
  26.2 9.0 %collective-permute-start.6 = (bf16[8,2,16,128]{3,2,1,0:T(8,128)(2,1)S(1)}, bf16[8,2,16,128]{3,2,1,0:T(8,128)(2,1)S(1)}, u32[]{:S(2)}, u32[]{:S(2)}) collective-permute-start(bf16[8,2,16,128]{3,2,1,0:T(8,128)(2,1)S(1)} %all-to-all-done.refs_5_), channel_id=1, source_target_pairs={{0,192},{64,128},{128,64},{192,0},{4,196},{68,132},{132,68},{196,4... | collective-permute-start | bytes 196616 | tf_op jit(solution)/shard_map/ppermute | solution.py:29
  28.7 6.5 %collective-permute-start.4 = (bf16[8,2,16,128]{3,2,1,0:T(8,128)(2,1)S(1)}, bf16[8,2,16,128]{3,2,1,0:T(8,128)(2,1)S(1)}, u32[]{:S(2)}, u32[]{:S(2)}) collective-permute-start(bf16[8,2,16,128]{3,2,1,0:T(8,128)(2,1)S(1)} %all-to-all-done.refs_5_), channel_id=1, source_target_pairs={{0,64},{64,0},{128,192},{192,128},{4,68},{68,4},{132,196},{196,132... | collective-permute-start | bytes 196616 | tf_op jit(solution)/shard_map/ppermute | solution.py:29
  28.8 6.4 %collective-permute-start.5 = (bf16[8,2,16,128]{3,2,1,0:T(8,128)(2,1)S(1)}, bf16[8,2,16,128]{3,2,1,0:T(8,128)(2,1)S(1)}, u32[]{:S(2)}, u32[]{:S(2)}) collective-permute-start(bf16[8,2,16,128]{3,2,1,0:T(8,128)(2,1)S(1)} %all-to-all-done.refs_5_), channel_id=1, source_target_pairs={{0,128},{64,192},{128,0},{192,64},{4,132},{68,196},{132,4},{196,68... | collective-permute-start | bytes 196616 | tf_op jit(solution)/shard_map/ppermute | solution.py:29
  35.0 26.5 %copy-start.3 = (bf16[2048,128]{1,0:T(8,128)(2,1)S(1)}, bf16[2048,128]{1,0:T(8,128)(2,1)}, u32[]{:S(2)}) copy-start(bf16[2048,128]{1,0:T(8,128)(2,1)} %label_ref.1) | copy-start | bytes 1572868
  35.1 26.5 %copy-start.4 = (f32[2048]{0:T(1024)S(1)}, f32[2048]{0:T(1024)}, u32[]{:S(2)}) copy-start(f32[2048]{0:T(1024)} %param.10) | copy-start | bytes 24580
  35.1 5.9 %collective-permute-start.3 = (bf16[4,2,4,32,128]{4,3,2,1,0:T(8,128)(2,1)S(1)}, bf16[4,2,4,32,128]{4,3,2,1,0:T(8,128)(2,1)S(1)}, u32[]{:S(2)}, u32[]{:S(2)}) collective-permute-start(bf16[4,2,4,32,128]{4,3,2,1,0:T(8,128)(2,1)S(1)} %pad_maximum_fusion), channel_id=1, source_target_pairs={{0,4},{4,0},{8,12},{12,8},{16,20},{20,16},{24,28},{28,24},{32,36},... | collective-permute-start | bytes 786440 | tf_op jit(solution)/shard_map/ppermute | solution.py:236
  36.0 5.0 %collective-permute-start.7 = (bf16[4,8,2,16,128]{4,3,2,1,0:T(8,128)(2,1)}, bf16[4,8,2,16,128]{4,3,2,1,0:T(8,128)(2,1)S(1)}, u32[]{:S(2)}, u32[]{:S(2)}) collective-permute-start(bf16[4,8,2,16,128]{4,3,2,1,0:T(8,128)(2,1)} %pad_maximum_fusion.1), channel_id=1, source_target_pairs={{0,4},{4,0},{8,12},{12,8},{16,20},{20,16},{24,28},{28,24},{32,36},... | collective-permute-start | bytes 786440 | tf_op jit(solution)/shard_map/ppermute | solution.py:241
  36.4 4.5 %copy-start.2 = (bf16[512,2048]{1,0:T(8,128)(2,1)S(1)}, bf16[512,2048]{1,0:T(8,128)(2,1)}, u32[]{:S(2)}) copy-start(bf16[512,2048]{1,0:T(8,128)(2,1)} %refs_10_.1) | copy-start | bytes 6291460
  45.1 9.7 %collective-permute-start.10 = (bf16[64,2048]{1,0:T(8,128)(2,1)}, bf16[64,2048]{1,0:T(8,128)(2,1)S(1)}, u32[]{:S(2)}, u32[]{:S(2)}) collective-permute-start(bf16[64,2048]{1,0:T(8,128)(2,1)} %get-tuple-element.22), channel_id=1, source_target_pairs={{0,3},{1,2},{2,1},{3,0},{4,7},{5,6},{6,5},{7,4},{8,11},{9,10},{10,... | collective-permute-start | bytes 786440 | tf_op jit(solution)/shard_map/ppermute | solution.py:281
  47.8 9.4 %collective-permute-start.8 = (bf16[64,2048]{1,0:T(8,128)(2,1)}, bf16[64,2048]{1,0:T(8,128)(2,1)S(1)}, u32[]{:S(2)}, u32[]{:S(2)}) collective-permute-start(bf16[64,2048]{1,0:T(8,128)(2,1)} %get-tuple-element.20), channel_id=1, source_target_pairs={{0,1},{1,0},{2,3},{3,2},{4,5},{5,4},{6,7},{7,6},{8,9},{9,8},{10,11... | collective-permute-start | bytes 786440 | tf_op jit(solution)/shard_map/ppermute | solution.py:281
  48.1 13.5 %collective-permute-start.9 = (bf16[64,2048]{1,0:T(8,128)(2,1)}, bf16[64,2048]{1,0:T(8,128)(2,1)S(1)}, u32[]{:S(2)}, u32[]{:S(2)}) collective-permute-start(bf16[64,2048]{1,0:T(8,128)(2,1)} %get-tuple-element.21), channel_id=1, source_target_pairs={{0,2},{1,3},{2,0},{3,1},{4,6},{5,7},{6,4},{7,5},{8,10},{9,11},{10,... | collective-permute-start | bytes 786440 | tf_op jit(solution)/shard_map/ppermute | solution.py:281
  61.9 4.8 %collective-permute-start.11 = (f32[64,128]{1,0:T(8,128)S(1)}, f32[64,128]{1,0:T(8,128)S(1)}, u32[]{:S(2)}, u32[]{:S(2)}) collective-permute-start(f32[64,128]{1,0:T(8,128)S(1)} %logits.1), channel_id=1, source_target_pairs={{0,1},{1,0},{2,3},{3,2},{4,5},{5,4},{6,7},{7,6},{8,9},{9,8},{10,11... | collective-permute-start | bytes 98312 | tf_op jit(solution)/shard_map/ppermute | solution.py:29
  62.2 6.2 %collective-permute-start.12 = (f32[64,128]{1,0:T(8,128)S(1)}, f32[64,128]{1,0:T(8,128)S(1)}, u32[]{:S(2)}, u32[]{:S(2)}) collective-permute-start(f32[64,128]{1,0:T(8,128)S(1)} %logits.1), channel_id=1, source_target_pairs={{0,2},{1,3},{2,0},{3,1},{4,6},{5,7},{6,4},{7,5},{8,10},{9,11},{10,... | collective-permute-start | bytes 98312 | tf_op jit(solution)/shard_map/ppermute | solution.py:29
  66.2 5.1 %collective-permute-start.13 = (f32[64,128]{1,0:T(8,128)S(1)}, f32[64,128]{1,0:T(8,128)S(1)}, u32[]{:S(2)}, u32[]{:S(2)}) collective-permute-start(f32[64,128]{1,0:T(8,128)S(1)} %logits.1), channel_id=1, source_target_pairs={{0,3},{1,2},{2,1},{3,0},{4,7},{5,6},{6,5},{7,4},{8,11},{9,10},{10,... | collective-permute-start | bytes 98312 | tf_op jit(solution)/shard_map/ppermute | solution.py:29
  (1 other events, 0.7 us)

commit v3 on v2

v3 whole, which is shorter than its diff:
```python
import functools

import jax
import jax.numpy as jnp
from jax import lax
from jax.experimental import pallas as pl
from jax.experimental.pallas import tpu as pltpu
from jax.sharding import PartitionSpec as P

SPAN = 8
PICKS = 40
LOW = -1e30
VMEM = pl.BlockSpec(memory_space=pltpu.VMEM)
HBM = pl.BlockSpec(memory_space=pltpu.HBM)
SMEM = pl.BlockSpec(memory_space=pltpu.SMEM)


def params(mib):
    return pltpu.CompilerParams(vmem_limit_bytes=mib << 20)


def segments(seq_count):
    return [
        [(SPAN * k - SPAN // 2 + i) % seq_count for i in range(SPAN)]
        for k in range(seq_count // SPAN)
    ]


def share(block, axis, groups):
    pieces = [block]
    for step in range(1, len(groups[0])):
        route = [(g[i], g[i ^ step]) for g in groups for i in range(len(g))]
        pieces.append(lax.ppermute(block, axis, route))
    return pieces


def dot(a, b):
    return jnp.dot(a, b, preferred_element_type=jnp.float32)


def dot_t(a, b):
    return lax.dot_general(a, b, (((1,), (1,)), ((), ())), preferred_element_type=jnp.float32)


def picked_rows(c, mid, far, mid_rows, seq_count):
    last = (c >= mid_rows) & (c < mid_rows + 4)
    other = jnp.where(last, (c - mid_rows) * seq_count + far, -1)
    return jnp.where(c < mid_rows, c * SPAN + mid, other)


def load_and_project(index, tok_hbm, w_hbm, tok_ref, w_ref, sems):
    deep = w_ref.shape[2]
    copies = {}
    count = 0
    for i, c in enumerate(index):
        for k in range(w_ref.shape[1]):
            rows = pl.ds(k * deep, deep)
            if i == 0:
                copies["t", k] = pltpu.make_async_copy(
                    tok_hbm.at[:, rows], tok_ref.at[k], sems.at[count]
                )
                count += 1
            copies[i, k] = pltpu.make_async_copy(
                w_hbm.at[c, rows], w_ref.at[i, k], sems.at[count]
            )
            count += 1
    for copy in copies.values():
        copy.start()

    def product(i):
        total = None
        for k in range(w_ref.shape[1]):
            if i == 0:
                copies["t", k].wait()
            copies[i, k].wait()
            part = dot(tok_ref[k], w_ref[i, k])
            total = part if total is None else total + part
        return total.astype(jnp.bfloat16)

    return product


def row_marks(mid, far, rows, seq_count):
    c = lax.broadcasted_iota(jnp.int32, (PICKS, rows), 0)
    r = lax.broadcasted_iota(jnp.int32, (PICKS, rows), 1)
    target = picked_rows(c, mid, far, rows // SPAN, seq_count)
    return jnp.where(r == target, 1.0, 0.0).astype(jnp.bfloat16)


def offset_copies(mid_hbm, far_hbm, mid_ref, far_ref, off_sems):
    offsets = [
        pltpu.make_async_copy(mid_hbm, mid_ref, off_sems.at[0]),
        pltpu.make_async_copy(far_hbm, far_ref, off_sems.at[1]),
    ]
    for copy in offsets:
        copy.start()
    return offsets


def kv_kernel(rows, heads, size, seq_count, mid_hbm, far_hbm, tok_hbm, w_hbm,
              kv_ref, mid_out, far_out, tok_ref, w_ref, few_ref, mid_ref, far_ref, off_sems, sems):
    offsets = offset_copies(mid_hbm, far_hbm, mid_ref, far_ref, off_sems)
    product = load_and_project((1, 2), tok_hbm, w_hbm, tok_ref, w_ref, sems)
    for copy in offsets:
        copy.wait()
    mid_rows = rows // SPAN
    marks = [row_marks(mid_ref[h], far_ref[h], rows, seq_count) for h in range(heads)]
    for c in range(2):
        whole = product(c)
        kv_ref[c] = whole
        for h in range(heads):
            got = dot(marks[h], whole[:, h * size : (h + 1) * size])
            for j in range(mid_out.shape[0]):
                mid_out[j, c, h] = got[:mid_rows].astype(jnp.bfloat16)
            few_ref[pl.ds(4 * h, 4)] = got[mid_rows : mid_rows + 4]
        few = few_ref[...].astype(jnp.bfloat16)
        for j in range(far_out.shape[0]):
            far_out[j, c] = few


def near_kernel(rows, heads, size, seq_count, mid_hbm, far_hbm, tok_hbm, w_hbm, kv_ref,
                near_ref, sel_ref, tok_ref, w_ref, mid_ref, far_ref, off_sems, sems):
    offsets = offset_copies(mid_hbm, far_hbm, mid_ref, far_ref, off_sems)
    product = load_and_project((0,), tok_hbm, w_hbm, tok_ref, w_ref, sems)
    whole = product(0)
    for copy in offsets:
        copy.wait()
    for h in range(heads):
        cols = slice(h * size, (h + 1) * size)
        queries = whole[:, cols]
        marks = row_marks(mid_ref[h], far_ref[h], rows, seq_count)
        sel_ref[h] = dot(marks, queries).astype(jnp.bfloat16)
        scores = dot_t(queries, kv_ref[0, :, cols]) * size**-0.5
        top = jnp.max(scores, axis=1, keepdims=True)
        weights = jnp.exp(scores - top)
        total = jnp.sum(weights, axis=1, keepdims=True)
        summed = dot(weights.astype(jnp.bfloat16), kv_ref[1, :, cols])
        near_ref[:, cols] = (summed / total).astype(jnp.bfloat16)


def softmax_parts(scores, values):
    top = jnp.max(scores, axis=1, keepdims=True)
    weights = jnp.exp(scores - top)
    total = jnp.sum(weights, axis=1, keepdims=True)
    return top, total, dot(weights.astype(jnp.bfloat16), values)


def wide_kernel(rows, heads, size, seq_count, quarters,
                mid_hbm, far_hbm, place_ref, sel_ref, kv_ref, near_ref, *refs):
    mid_lines, far_lines, w_hbm = refs[0:2], refs[2:4], refs[4]
    outs, attn_ref = refs[5 : 5 + quarters], refs[5 + quarters]
    mid_ref, far_ref, off_sems, w_ref, w_sem = refs[6 + quarters :]
    offsets = offset_copies(mid_hbm, far_hbm, mid_ref, far_ref, off_sems)
    w_copy = pltpu.make_async_copy(w_hbm, w_ref, w_sem)
    w_copy.start()
    mid_rows = rows // SPAN
    scale = size**-0.5
    far_rows = lambda i: jnp.concatenate([ref[:, i].reshape(-1, size) for ref in far_lines])
    far_q = jnp.concatenate([sel_ref[h].astype(jnp.float32)[mid_rows:] for h in range(heads)])
    far_scores = dot_t(far_q.astype(jnp.bfloat16), far_rows(0)) * scale
    q_head = lax.broadcasted_iota(jnp.int32, far_scores.shape, 0) // 8
    k_head = (lax.broadcasted_iota(jnp.int32, far_scores.shape, 1) % 16) // 4
    far_top, far_total, far_sum = softmax_parts(
        jnp.where(q_head == k_head, far_scores, LOW), far_rows(1)
    )
    for copy in offsets:
        copy.wait()
    for h in range(heads):
        cols = slice(h * size, (h + 1) * size)
        mid_off, far_off = mid_ref[h], far_ref[h]
        stack = lambda i: jnp.concatenate(
            [kv_ref[i, :, cols]] + [ref[:, i, h].reshape(-1, size) for ref in mid_lines]
        )
        scores = dot_t(sel_ref[h], stack(0)) * scale
        row = lax.broadcasted_iota(jnp.int32, scores.shape, 0)
        col = lax.broadcasted_iota(jnp.int32, scores.shape, 1)
        both = ((far_off + SPAN - mid_off) & (SPAN - 1)) == 0
        keep = (row < mid_rows) | (col < rows) | both
        top, total, summed = softmax_parts(jnp.where(keep, scores, LOW), stack(1))
        attn = summed / total
        far = slice(8 * h, 8 * h + 8)
        peak = jnp.maximum(top[mid_rows:], far_top[far])
        mine = jnp.exp(top[mid_rows:] - peak)
        other = jnp.exp(far_top[far] - peak)
        attn_far = (mine * summed[mid_rows:] + other * far_sum[far]) / (
            mine * total[mid_rows:] + other * far_total[far]
        )
        attn = jnp.concatenate([attn[:mid_rows], attn_far]).astype(jnp.bfloat16)
        r = lax.broadcasted_iota(jnp.int32, (rows, PICKS), 0)
        c = lax.broadcasted_iota(jnp.int32, (rows, PICKS), 1)
        target = picked_rows(c, mid_off, far_off, mid_rows, seq_count)
        twice = (c < mid_rows) & (
            ((target + seq_count - far_off) & (seq_count - 1)) == 0
        )
        marks = jnp.where((r == target) & jnp.logical_not(twice), 1.0, 0.0)
        hit = jnp.sum(marks, axis=1, keepdims=True) > 0.5
        put = dot(marks.astype(jnp.bfloat16), attn)
        attn_ref[:, cols] = jnp.where(hit, put, near_ref[:, cols].astype(jnp.float32))
    own = rows // quarters
    place = place_ref[0]
    order = jnp.concatenate(
        [
            attn_ref[pl.ds(pl.multiple_of((place ^ s) * own, own), own), :]
            for s in range(quarters)
        ]
    ).astype(jnp.bfloat16)
    w_copy.wait()
    chunk = 512
    for start in range(0, w_ref.shape[1], chunk):
        part = dot(order, w_ref[:, start : start + chunk]).astype(jnp.bfloat16)
        for s in range(quarters):
            outs[s][:, start : start + chunk] = part[s * own : (s + 1) * own]


def logits_kernel(place_ref, tok_ref, gain_ref, label_ref, *refs):
    out_ref = refs[-1]
    mixed = tok_ref[...].astype(jnp.float32)
    for ref in refs[:-1]:
        mixed = mixed + ref[...].astype(jnp.float32)
    mean_sq = jnp.mean(mixed * mixed, axis=1, keepdims=True)
    scaled = (mixed * gain_ref[...]).astype(jnp.bfloat16)
    out_ref[...] = dot(scaled, label_ref[...]) / jnp.sqrt(mean_sq + 1e-05)


def body(tokens, w_qkv, w_out, norm_gain, w_label, offset_mid, offset_far):
    rows, width = tokens.shape
    heads = offset_mid.shape[0]
    cols = w_qkv.shape[2]
    size = cols // heads
    seq_count = lax.axis_size("seq")
    head_count = lax.axis_size("head")
    place = lax.axis_index("head")
    mid_rows = rows // SPAN
    sizes = (rows, heads, size, seq_count)
    bf16 = lambda *shape: jax.ShapeDtypeStruct(shape, jnp.bfloat16)
    stay = lambda a: pltpu.with_memory_space_constraint(a, pltpu.HBM)
    tokens, weights = stay(tokens), stay(w_qkv.transpose(1, 0, 2))
    offset_mid, offset_far, w_out = stay(offset_mid), stay(offset_far), stay(w_out)
    deep = 512

    groups = segments(seq_count)
    across = [[g[2 * i + c] for i in range(SPAN // 2)] for g in groups for c in range(2)]
    chips = [list(range(c, seq_count, 2)) for c in range(2)]
    cores = [(i, i ^ 1) for i in range(seq_count)]
    near_count, far_count = len(across[0]), len(chips[0])
    steps = width // deep
    tok_scratch = pltpu.VMEM((steps, rows, deep), jnp.bfloat16)

    off_scratch = [
        pltpu.SMEM((heads,), jnp.int32),
        pltpu.SMEM((heads,), jnp.int32),
        pltpu.SemaphoreType.DMA((2,)),
    ]

    kv, mid_kv, far_kv = pl.pallas_call(
        functools.partial(kv_kernel, *sizes),
        in_specs=[HBM] * 4,
        out_specs=[VMEM] * 3,
        out_shape=[
            bf16(2, rows, cols),
            bf16(1, 2, heads, mid_rows, size),
            bf16(far_count, 2, 4 * heads, size),
        ],
        scratch_shapes=[
            tok_scratch,
            pltpu.VMEM((2, steps, deep, cols), jnp.bfloat16),
            pltpu.VMEM((4 * heads, size), jnp.float32),
            *off_scratch,
            pltpu.SemaphoreType.DMA((3 * steps,)),
        ],
        compiler_params=params(20),
        name="keys_values",
    )(offset_mid, offset_far, tokens, weights)

    far_line = lax.all_to_all(far_kv, "seq", 0, 0, axis_index_groups=chips)
    mid_pieces = share(mid_kv[0], "seq", across)
    near, sel = pl.pallas_call(
        functools.partial(near_kernel, *sizes),
        in_specs=[HBM] * 4 + [VMEM],
        out_specs=[VMEM] * 2,
        out_shape=[bf16(rows, cols), bf16(heads, PICKS, size)],
        scratch_shapes=[
            tok_scratch,
            pltpu.VMEM((1, steps, deep, cols), jnp.bfloat16),
            *off_scratch,
            pltpu.SemaphoreType.DMA((2 * steps,)),
        ],
        compiler_params=params(14),
        name="near",
    )(offset_mid, offset_far, tokens, weights, kv)

    *mid_pieces, near = lax.optimization_barrier((*mid_pieces, near))
    mid_line = jnp.stack(mid_pieces)
    mid_other = lax.ppermute(mid_line, "seq", cores)
    far_other = lax.ppermute(far_line, "seq", cores)

    own = rows // head_count
    place_arr = place.astype(jnp.int32).reshape(1)
    parts = pl.pallas_call(
        functools.partial(wide_kernel, *sizes, head_count),
        in_specs=[HBM, HBM, SMEM] + [VMEM] * 7 + [HBM],
        out_specs=[VMEM] * head_count,
        out_shape=[bf16(own, width)] * head_count,
        scratch_shapes=[
            pltpu.VMEM((rows, cols), jnp.float32),
            *off_scratch,
            pltpu.VMEM(w_out.shape, jnp.bfloat16),
            pltpu.SemaphoreType.DMA,
        ],
        compiler_params=params(14),
        name="wide",
    )(
        offset_mid, offset_far, place_arr, sel, kv, near,
        mid_line, mid_other, far_line, far_other, w_out,
    )

    got = [parts[0]]
    for step in range(1, head_count):
        route = [(i, i ^ step) for i in range(head_count)]
        got.append(lax.ppermute(parts[step], "head", route))

    whole = lambda *shape: pl.BlockSpec(shape, lambda i, p: (0,) * len(shape))
    logit = pl.pallas_call(
        logits_kernel,
        grid_spec=pltpu.PrefetchScalarGridSpec(
            num_scalar_prefetch=1,
            grid=(1,),
            in_specs=[
                pl.BlockSpec((own, width), lambda i, p: (p[0], 0)),
                whole(1, width),
                whole(*w_label.shape),
            ]
            + [whole(own, width)] * head_count,
            out_specs=whole(own, w_label.shape[1]),
        ),
        out_shape=jax.ShapeDtypeStruct((own, w_label.shape[1]), jnp.float32),
        compiler_params=params(10),
        name="logits",
    )(place_arr, tokens, norm_gain.reshape(1, width), w_label, *got)

    every = share(logit, "head", [list(range(head_count))])
    logits = jnp.zeros((head_count,) + logit.shape, jnp.float32)
    for step in range(head_count):
        logits = lax.dynamic_update_index_in_dim(logits, every[step], place ^ step, 0)
    return logits.reshape(rows, -1)


def solution(mesh):
    return jax.shard_map(
        body,
        mesh=mesh,
        in_specs=(
            P("seq", None),
            P(None, None, "head"),
            P("head", None),
            P(),
            P(),
            P("head"),
            P("head"),
        ),
        out_specs=P("seq", None),
        check_vma=False,
    )
```

time: 73 us -> 65.8 us (0.901)
  Pallas kernels: 15.6 us -> 12.1 us
  local copies, waits for them, and re-layouts: 3.92 us -> 0.7 us
  waiting for transfers between devices: 20.5 us -> 22.4 us
  starting transfers between devices: 31 us -> 29.3 us
  other arithmetic: 0.79 us -> 0.04 us
    ppermute x9 -> x6, starting transfers between devices: 17.2 us -> 12.6 us  [share(): pieces.append(lax.ppermute(block, axis, route))]
    pallas_call x2, Pallas kernels: 11.2 us -> 7.73 us  [the longest x1 4.21 us: body(): pl.pallas_call(functools.partial(kv_kernel, *sizes), in_specs=[HBM] * 4,...]
    all_to_all x1, starting transfers between devices: 8.57 us -> 11.4 us  [body(): far_line = lax.all_to_all(far_kv, 'seq', 0, 0, axis_index_groups=chips)]
    unnamed x20 -> x6, local copies, waits for them, and re-layouts: 3.24 us -> 0.67 us
    ppermute x3, waiting for transfers between devices: 11.8 us -> 14.1 us  [body(): got.append(lax.ppermute(parts[step], 'head', route))]
    ppermute x9 -> x6, waiting for transfers between devices: 8.71 us -> 6.84 us  [share(): pieces.append(lax.ppermute(block, axis, route))]
    ppermute x2, waiting for transfers between devices: 0.01 us -> 1.4 us  [the longest x1 1.02 us: body(): mid_other = lax.ppermute(mid_line, 'seq', cores)]
    pallas_call x1, Pallas kernels: 4.1 us -> 3.1 us  [body(): pl.pallas_call(functools.partial(wide_kernel, *sizes, head_count), in_spe...]
  transfers between devices with their start and end apart: 15 -> 12, of which waited for: 6 -> 9; matrix products, arithmetic and copies ran while one was open for 1% -> 0% of each run, Pallas kernels for 6% -> 5%
where the time goes in v3:
time: 65.8 us; the launch traced here: 64.7 us
  starting transfers between devices  29.3 us (45%)
  waiting for transfers between devices  22.4 us (34%)
  Pallas kernels  12.1 us (18%)
  local copies, waits for them, and re-layouts  0.7 us (1%)
    ppermute x3, waiting for transfers between devices, body(): got.append(lax.ppermute(parts[step], 'head', route))  14.1 us
    ppermute x6, starting transfers between devices, share(): pieces.append(lax.ppermute(block, axis, route))  12.6 us
    all_to_all x1, starting transfers between devices, body(): far_line = lax.all_to_all(far_kv, 'seq', 0, 0, axis_index_groups=chips)  11.4 us
    ppermute x6, waiting for transfers between devices, share(): pieces.append(lax.ppermute(block, axis, route))  6.84 us
    ppermute x3, starting transfers between devices, body(): got.append(lax.ppermute(parts[step], 'head', route))  4.79 us
    pallas_call x1, Pallas kernels, body(): pl.pallas_call(functools.partial(kv_kernel, *sizes), in_specs=[HBM] * 4,...  4.21 us
    pallas_call x1, Pallas kernels, body(): pl.pallas_call(functools.partial(near_kernel, *sizes), in_specs=[HBM] * 4...  3.52 us
    pallas_call x1, Pallas kernels, body(): pl.pallas_call(functools.partial(wide_kernel, *sizes, head_count), in_spe...  3.1 us
  transfers between devices with their start and end apart: 12, of which 9 were waited for; matrix products, arithmetic and copies ran while one was open for 0% of the time, Pallas kernels for 5%

profile of v3, /device:TPU:32, one launch (start us, length us, event | category | flops | bytes accessed | tf_op | source)
XLA Modules:
  0.0 64.7 jit_solution(4623870138067661908)
XLA Ops:
  0.0 4.2 %keys_values.1 = (bf16[2,256,512]{2,1,0:T(8,128)(2,1)S(1)}, bf16[1,2,4,32,128]{4,3,2,1,0:T(8,128)(2,1)S(1)}, bf16[32,2,16,128]{3,2,1,0:T(8,128)(2,1)}) custom-call(s32[4]{0:T(128)} %mid_hbm.5, s32[4]{0:T(128)} %far_hbm.5, bf16[256,2048]{1,0:T(8,128)(2,1)} %tok_ref.1, bf16[3,2048,512]{2,1,0:T(8,128)(2,1)} %bitcast.21), custom_call_target="tpu_custom_call" | custom-call | tf_op jit(solution)/shard_map/keys_values/pallas_call | solution.py:255
  4.2 11.4 %all-to-all-start = ((bf16[32,2,16,128]{3,2,1,0:T(8,128)(2,1)}), bf16[32,2,16,128]{3,2,1,0:T(8,128)(2,1)S(1)}, u32[]{:S(2)}, u32[]{:S(2)}) async-start(bf16[32,2,16,128]{3,2,1,0:T(8,128)(2,1)} %get-tuple-element.28), calls=%async_computation | async-start | bytes 524288 | tf_op jit(solution)/shard_map/all_to_all | solution.py:275
  15.6 0.3 collective-permute-start
  15.9 6.1 %collective-permute-start.1 = (bf16[2,4,32,128]{3,2,1,0:T(8,128)(2,1)S(1)}, bf16[2,4,32,128]{3,2,1,0:T(8,128)(2,1)S(1)}, u32[]{:S(2)}, u32[]{:S(2)}) collective-permute-start(bf16[2,4,32,128]{3,2,1,0:T(8,128)(2,1)S(1)} %bitcast.18), channel_id=1, source_target_pairs={{240,0},{248,8},{0,240},{8,248},{244,4},{252,12},{4,244},{12,252},... | collective-permute-start | bytes 196616 | tf_op jit(solution)/shard_map/ppermute | solution.py:33
  22.0 1.4 %collective-permute-start.2 = (bf16[2,4,32,128]{3,2,1,0:T(8,128)(2,1)S(1)}, bf16[2,4,32,128]{3,2,1,0:T(8,128)(2,1)S(1)}, u32[]{:S(2)}, u32[]{:S(2)}) collective-permute-start(bf16[2,4,32,128]{3,2,1,0:T(8,128)(2,1)S(1)} %bitcast.19), channel_id=1, source_target_pairs={{240,8},{248,0},{0,248},{8,240},{244,12},{252,4},{4,252},{12,244},... | collective-permute-start | bytes 196616 | tf_op jit(solution)/shard_map/ppermute | solution.py:33
  23.4 3.5 %near.1 = (bf16[256,512]{1,0:T(8,128)(2,1)S(1)}, bf16[4,40,128]{2,1,0:T(8,128)(2,1)S(1)}) custom-call(s32[4]{0:T(128)} %mid_hbm.5, s32[4]{0:T(128)} %far_hbm.5, bf16[256,2048]{1,0:T(8,128)(2,1)} %tok_ref.1, bf16[3,2048,512]{2,1,0:T(8,128)(2,1)} %bitcast.22, bf16[2,256,512]{2,1,0:T(8,128)(2,1)S(1)} %get-tuple-element.19.kv_ref), custom_call_target="tpu_custom_call" | custom-call | tf_op jit(solution)/shard_map/near/pallas_call | solution.py:277
  27.0 0.1 collective-permute-done.1
  27.1 4.4 %collective-permute-done.2 = bf16[2,4,32,128]{3,2,1,0:T(8,128)(2,1)S(1)} collective-permute-done((bf16[2,4,32,128]{3,2,1,0:T(8,128)(2,1)S(1)}, bf16[2,4,32,128]{3,2,1,0:T(8,128)(2,1)S(1)}, u32[]{:S(2)}, u32[]{:S(2)}) %collective-permute-start.2) | collective-permute-done | bytes 65568 | tf_op jit(solution)/shard_map/ppermute | solution.py:33
  31.6 0.5 collective-permute-start.4
  32.1 1.0 %collective-permute-done.3.refs_1_ = bf16[4,2,4,32,128]{4,3,2,1,0:T(8,128)(2,1)S(1)} collective-permute-done((bf16[4,2,4,32,128]{4,3,2,1,0:T(8,128)(2,1)S(1)}, bf16[4,2,4,32,128]{4,3,2,1,0:T(8,128)(2,1)S(1)}, u32[]{:S(2)}, u32[]{:S(2)}) %collective-permute-start.3) | collective-permute-done | bytes 262176 | tf_op jit(solution)/shard_map/ppermute | solution.py:294
  33.1 0.4 collective-permute-done.4.refs_3_
  33.5 3.1 %wide.1 = (bf16[64,2048]{1,0:T(8,128)(2,1)S(1)}, bf16[64,2048]{1,0:T(8,128)(2,1)S(1)}, bf16[64,2048]{1,0:T(8,128)(2,1)S(1)}, bf16[64,2048]{1,0:T(8,128)(2,1)S(1)}) custom-call(s32[4]{0:T(128)} %mid_hbm.5, s32[4]{0:T(128)} %far_hbm.5, s32[1]{0:T(128)} %bitcast.place_ref, bf16[4,40,128]{2,1,0:T(8,128)(2,1)S(1)} %get-tuple-element.20.sel_ref, ...), custom_call_target="tpu_custom_call" | custom-call | tf_op jit(solution)/shard_map/wide/pallas_call | solution.py:299
  36.6 1.6 %collective-permute-start.5 = (bf16[64,2048]{1,0:T(8,128)(2,1)S(1)}, bf16[64,2048]{1,0:T(8,128)(2,1)S(1)}, u32[]{:S(2)}, u32[]{:S(2)}) collective-permute-start(bf16[64,2048]{1,0:T(8,128)(2,1)S(1)} %get-tuple-element.30), channel_id=1, source_target_pairs={{0,1},{1,0},{2,3},{3,2},{4,5},{5,4},{6,7},{7,6},{8,9},{9,8},{10,11... | collective-permute-start | bytes 786440 | tf_op jit(solution)/shard_map/ppermute | solution.py:320
  38.2 2.7 %collective-permute-start.6 = (bf16[64,2048]{1,0:T(8,128)(2,1)S(1)}, bf16[64,2048]{1,0:T(8,128)(2,1)S(1)}, u32[]{:S(2)}, u32[]{:S(2)}) collective-permute-start(bf16[64,2048]{1,0:T(8,128)(2,1)S(1)} %get-tuple-element.31), channel_id=1, source_target_pairs={{0,2},{1,3},{2,0},{3,1},{4,6},{5,7},{6,4},{7,5},{8,10},{9,11},{10,... | collective-permute-start | bytes 786440 | tf_op jit(solution)/shard_map/ppermute | solution.py:320
  40.9 0.5 collective-permute-start.7
  41.4 4.5 %collective-permute-done.5.refs_1_ = bf16[64,2048]{1,0:T(8,128)(2,1)S(1)} collective-permute-done((bf16[64,2048]{1,0:T(8,128)(2,1)S(1)}, bf16[64,2048]{1,0:T(8,128)(2,1)S(1)}, u32[]{:S(2)}, u32[]{:S(2)}) %collective-permute-start.5) | collective-permute-done | bytes 262176 | tf_op jit(solution)/shard_map/ppermute | solution.py:320
  45.9 7.1 %collective-permute-done.6.refs_2_ = bf16[64,2048]{1,0:T(8,128)(2,1)S(1)} collective-permute-done((bf16[64,2048]{1,0:T(8,128)(2,1)S(1)}, bf16[64,2048]{1,0:T(8,128)(2,1)S(1)}, u32[]{:S(2)}, u32[]{:S(2)}) %collective-permute-start.6) | collective-permute-done | bytes 262176 | tf_op jit(solution)/shard_map/ppermute | solution.py:320
  53.0 2.6 %collective-permute-done.7.refs_3_ = bf16[64,2048]{1,0:T(8,128)(2,1)S(1)} collective-permute-done((bf16[64,2048]{1,0:T(8,128)(2,1)S(1)}, bf16[64,2048]{1,0:T(8,128)(2,1)S(1)}, u32[]{:S(2)}, u32[]{:S(2)}) %collective-permute-start.7) | collective-permute-done | bytes 262176 | tf_op jit(solution)/shard_map/ppermute | solution.py:320
  55.6 1.3 %logits.1 = f32[64,128]{1,0:T(8,128)S(1)} custom-call(s32[1]{0:T(128)} %bitcast.place_ref, bf16[256,2048]{1,0:T(8,128)(2,1)} %tok_ref.1, f32[1,2048]{1,0:T(1,128)S(1)} %bitcast.20, bf16[2048,128]{1,0:T(8,128)(2,1)S(1)} %copy-done, bf16[64,2048]{1,0:T(8,128)(2,1)S(1)} %get-tuple-element.29.refs_0_, bf16[64,2048]{1,0:T(8,128)(2,1)S(1)} %collective-permute-done.5.refs_1_, ...), custom_call_target="tpu_custom_call" | custom-call | tf_op jit(solution)/shard_map/logits/pallas_call | solution.py:323
  56.9 1.9 %collective-permute-start.9 = (f32[64,128]{1,0:T(8,128)S(1)}, f32[64,128]{1,0:T(8,128)S(1)}, u32[]{:S(2)}, u32[]{:S(2)}) collective-permute-start(f32[64,128]{1,0:T(8,128)S(1)} %logits.1), channel_id=1, source_target_pairs={{0,2},{1,3},{2,0},{3,1},{4,6},{5,7},{6,4},{7,5},{8,10},{9,11},{10,... | collective-permute-start | bytes 98312 | tf_op jit(solution)/shard_map/ppermute | solution.py:33
  58.9 2.8 %collective-permute-start.10 = (f32[64,128]{1,0:T(8,128)S(1)}, f32[64,128]{1,0:T(8,128)S(1)}, u32[]{:S(2)}, u32[]{:S(2)}) collective-permute-start(f32[64,128]{1,0:T(8,128)S(1)} %logits.1), channel_id=1, source_target_pairs={{0,3},{1,2},{2,1},{3,0},{4,7},{5,6},{6,5},{7,4},{8,11},{9,10},{10,... | collective-permute-start | bytes 98312 | tf_op jit(solution)/shard_map/ppermute | solution.py:33
  61.7 0.8 %collective-permute-done.9 = f32[64,128]{1,0:T(8,128)S(1)} collective-permute-done((f32[64,128]{1,0:T(8,128)S(1)}, f32[64,128]{1,0:T(8,128)S(1)}, u32[]{:S(2)}, u32[]{:S(2)}) %collective-permute-start.9) | collective-permute-done | bytes 32800 | tf_op jit(solution)/shard_map/ppermute | solution.py:33
  62.5 1.5 %collective-permute-done.10 = f32[64,128]{1,0:T(8,128)S(1)} collective-permute-done((f32[64,128]{1,0:T(8,128)S(1)}, f32[64,128]{1,0:T(8,128)S(1)}, u32[]{:S(2)}, u32[]{:S(2)}) %collective-permute-start.10) | collective-permute-done | bytes 32800 | tf_op jit(solution)/shard_map/ppermute | solution.py:33
  64.0 0.7 %copy-done.2 = f32[4,64,128]{2,1,0:T(8,128)} copy-done((f32[4,64,128]{2,1,0:T(8,128)}, f32[4,64,128]{2,1,0:T(8,128)S(1)}, u32[]{:S(2)}) %copy-start.2) | copy-done | bytes 131096
  (16 shorter events, 0.3 us)
Async XLA Ops:
  4.2 27.4 %all-to-all-start = ((bf16[32,2,16,128]{3,2,1,0:T(8,128)(2,1)}), bf16[32,2,16,128]{3,2,1,0:T(8,128)(2,1)S(1)}, u32[]{:S(2)}, u32[]{:S(2)}) async-start(bf16[32,2,16,128]{3,2,1,0:T(8,128)(2,1)} %get-tuple-element.28), calls=%async_computation | async-start | bytes 524288 | tf_op jit(solution)/shard_map/all_to_all | solution.py:275
  15.6 40.0 %copy-start = (bf16[2048,128]{1,0:T(8,128)(2,1)S(1)}, bf16[2048,128]{1,0:T(8,128)(2,1)}, u32[]{:S(2)}) copy-start(bf16[2048,128]{1,0:T(8,128)(2,1)} %label_ref.1) | copy-start | bytes 1572868
  15.6 40.0 %copy-start.1 = (f32[2048]{0:T(1024)S(1)}, f32[2048]{0:T(1024)}, u32[]{:S(2)}) copy-start(f32[2048]{0:T(1024)} %param.10) | copy-start | bytes 24580
  15.6 11.3 %collective-permute-start = (bf16[2,4,32,128]{3,2,1,0:T(8,128)(2,1)S(1)}, bf16[2,4,32,128]{3,2,1,0:T(8,128)(2,1)S(1)}, u32[]{:S(2)}, u32[]{:S(2)}) collective-permute-start(bf16[2,4,32,128]{3,2,1,0:T(8,128)(2,1)S(1)} %bitcast.17), channel_id=1, source_target_pairs={{240,248},{248,240},{0,8},{8,0},{244,252},{252,244},{4,12},{12,4},... | collective-permute-start | bytes 196616 | tf_op jit(solution)/shard_map/ppermute | solution.py:33
  15.9 11.1 %collective-permute-start.1 = (bf16[2,4,32,128]{3,2,1,0:T(8,128)(2,1)S(1)}, bf16[2,4,32,128]{3,2,1,0:T(8,128)(2,1)S(1)}, u32[]{:S(2)}, u32[]{:S(2)}) collective-permute-start(bf16[2,4,32,128]{3,2,1,0:T(8,128)(2,1)S(1)} %bitcast.18), channel_id=1, source_target_pairs={{240,0},{248,8},{0,240},{8,248},{244,4},{252,12},{4,244},{12,252},... | collective-permute-start | bytes 196616 | tf_op jit(solution)/shard_map/ppermute | solution.py:33
  22.0 9.5 %collective-permute-start.2 = (bf16[2,4,32,128]{3,2,1,0:T(8,128)(2,1)S(1)}, bf16[2,4,32,128]{3,2,1,0:T(8,128)(2,1)S(1)}, u32[]{:S(2)}, u32[]{:S(2)}) collective-permute-start(bf16[2,4,32,128]{3,2,1,0:T(8,128)(2,1)S(1)} %bitcast.19), channel_id=1, source_target_pairs={{240,8},{248,0},{0,248},{8,240},{244,12},{252,4},{4,252},{12,244},... | collective-permute-start | bytes 196616 | tf_op jit(solution)/shard_map/ppermute | solution.py:33
  31.5 1.6 %collective-permute-start.3 = (bf16[4,2,4,32,128]{4,3,2,1,0:T(8,128)(2,1)S(1)}, bf16[4,2,4,32,128]{4,3,2,1,0:T(8,128)(2,1)S(1)}, u32[]{:S(2)}, u32[]{:S(2)}) collective-permute-start(bf16[4,2,4,32,128]{4,3,2,1,0:T(8,128)(2,1)S(1)} %pad_maximum_fusion.refs_0_), channel_id=1, source_target_pairs={{0,4},{4,0},{8,12},{12,8},{16,20},{20,16},{24,28},{28,24},{32,36},... | collective-permute-start | bytes 786440 | tf_op jit(solution)/shard_map/ppermute | solution.py:294
  31.6 1.9 %collective-permute-start.4 = (bf16[32,2,16,128]{3,2,1,0:T(8,128)(2,1)S(1)}, bf16[32,2,16,128]{3,2,1,0:T(8,128)(2,1)S(1)}, u32[]{:S(2)}, u32[]{:S(2)}) collective-permute-start(bf16[32,2,16,128]{3,2,1,0:T(8,128)(2,1)S(1)} %all-to-all-done.refs_2_), channel_id=1, source_target_pairs={{0,4},{4,0},{8,12},{12,8},{16,20},{20,16},{24,28},{28,24},{32,36},... | collective-permute-start | bytes 786440 | tf_op jit(solution)/shard_map/ppermute | solution.py:295
  36.6 9.2 %collective-permute-start.5 = (bf16[64,2048]{1,0:T(8,128)(2,1)S(1)}, bf16[64,2048]{1,0:T(8,128)(2,1)S(1)}, u32[]{:S(2)}, u32[]{:S(2)}) collective-permute-start(bf16[64,2048]{1,0:T(8,128)(2,1)S(1)} %get-tuple-element.30), channel_id=1, source_target_pairs={{0,1},{1,0},{2,3},{3,2},{4,5},{5,4},{6,7},{7,6},{8,9},{9,8},{10,11... | collective-permute-start | bytes 786440 | tf_op jit(solution)/shard_map/ppermute | solution.py:320
  38.2 14.8 %collective-permute-start.6 = (bf16[64,2048]{1,0:T(8,128)(2,1)S(1)}, bf16[64,2048]{1,0:T(8,128)(2,1)S(1)}, u32[]{:S(2)}, u32[]{:S(2)}) collective-permute-start(bf16[64,2048]{1,0:T(8,128)(2,1)S(1)} %get-tuple-element.31), channel_id=1, source_target_pairs={{0,2},{1,3},{2,0},{3,1},{4,6},{5,7},{6,4},{7,5},{8,10},{9,11},{10,... | collective-permute-start | bytes 786440 | tf_op jit(solution)/shard_map/ppermute | solution.py:320
  40.9 14.6 %collective-permute-start.7 = (bf16[64,2048]{1,0:T(8,128)(2,1)S(1)}, bf16[64,2048]{1,0:T(8,128)(2,1)S(1)}, u32[]{:S(2)}, u32[]{:S(2)}) collective-permute-start(bf16[64,2048]{1,0:T(8,128)(2,1)S(1)} %get-tuple-element.32), channel_id=1, source_target_pairs={{0,3},{1,2},{2,1},{3,0},{4,7},{5,6},{6,5},{7,4},{8,11},{9,10},{10,... | collective-permute-start | bytes 786440 | tf_op jit(solution)/shard_map/ppermute | solution.py:320
  56.8 4.8 %collective-permute-start.8 = (f32[64,128]{1,0:T(8,128)S(1)}, f32[64,128]{1,0:T(8,128)S(1)}, u32[]{:S(2)}, u32[]{:S(2)}) collective-permute-start(f32[64,128]{1,0:T(8,128)S(1)} %logits.1), channel_id=1, source_target_pairs={{0,1},{1,0},{2,3},{3,2},{4,5},{5,4},{6,7},{7,6},{8,9},{9,8},{10,11... | collective-permute-start | bytes 98312 | tf_op jit(solution)/shard_map/ppermute | solution.py:33
  56.9 5.5 %collective-permute-start.9 = (f32[64,128]{1,0:T(8,128)S(1)}, f32[64,128]{1,0:T(8,128)S(1)}, u32[]{:S(2)}, u32[]{:S(2)}) collective-permute-start(f32[64,128]{1,0:T(8,128)S(1)} %logits.1), channel_id=1, source_target_pairs={{0,2},{1,3},{2,0},{3,1},{4,6},{5,7},{6,4},{7,5},{8,10},{9,11},{10,... | collective-permute-start | bytes 98312 | tf_op jit(solution)/shard_map/ppermute | solution.py:33
  58.9 5.1 %collective-permute-start.10 = (f32[64,128]{1,0:T(8,128)S(1)}, f32[64,128]{1,0:T(8,128)S(1)}, u32[]{:S(2)}, u32[]{:S(2)}) collective-permute-start(f32[64,128]{1,0:T(8,128)S(1)} %logits.1), channel_id=1, source_target_pairs={{0,3},{1,2},{2,1},{3,0},{4,7},{5,6},{6,5},{7,4},{8,11},{9,10},{10,... | collective-permute-start | bytes 98312 | tf_op jit(solution)/shard_map/ppermute | solution.py:33
  64.0 0.7 %copy-start.2 = (f32[4,64,128]{2,1,0:T(8,128)}, f32[4,64,128]{2,1,0:T(8,128)S(1)}, u32[]{:S(2)}) copy-start(f32[4,64,128]{2,1,0:T(8,128)S(1)} %bitcast_dynamic-update-slice_fusion) | copy-start | bytes 393220

commit v4 on v3

--- a/solution.py
+++ b/solution.py
@@ -10,6 +10,7 @@
 SPAN = 8
 PICKS = 40
 LOW = -1e30
+HALVING = (((0, 3), (1, 2)), ((0, 1), (3, 2)))
 VMEM = pl.BlockSpec(memory_space=pltpu.VMEM)
 HBM = pl.BlockSpec(memory_space=pltpu.HBM)
 SMEM = pl.BlockSpec(memory_space=pltpu.SMEM)
@@ -148,8 +149,8 @@
 def wide_kernel(rows, heads, size, seq_count, quarters,
                 mid_hbm, far_hbm, place_ref, sel_ref, kv_ref, near_ref, *refs):
     mid_lines, far_lines, w_hbm = refs[0:2], refs[2:4], refs[4]
-    outs, attn_ref = refs[5 : 5 + quarters], refs[5 + quarters]
-    mid_ref, far_ref, off_sems, w_ref, w_sem = refs[6 + quarters :]
+    outs, refs = refs[5:9], refs[9:]
+    attn_ref, mid_ref, far_ref, off_sems, w_ref, w_sem = refs
     offsets = offset_copies(mid_hbm, far_hbm, mid_ref, far_ref, off_sems)
     w_copy = pltpu.make_async_copy(w_hbm, w_ref, w_sem)
     w_copy.start()
@@ -205,21 +206,32 @@
         ]
     ).astype(jnp.bfloat16)
     w_copy.wait()
+    half = w_ref.shape[1] // 2
     chunk = 512
-    for start in range(0, w_ref.shape[1], chunk):
+    for start in range(0, 2 * half, chunk):
         part = dot(order, w_ref[:, start : start + chunk]).astype(jnp.bfloat16)
-        for s in range(quarters):
-            outs[s][:, start : start + chunk] = part[s * own : (s + 1) * own]
+        side = start // half
+        to = slice(start % half, start % half + chunk)
+        for name, taken in enumerate(HALVING[side]):
+            for i, s in enumerate(taken):
+                outs[2 * side + name][i * own : (i + 1) * own, to] = part[s * own : (s + 1) * own]
 
 
 def logits_kernel(place_ref, tok_ref, gain_ref, label_ref, *refs):
     out_ref = refs[-1]
-    mixed = tok_ref[...].astype(jnp.float32)
-    for ref in refs[:-1]:
-        mixed = mixed + ref[...].astype(jnp.float32)
-    mean_sq = jnp.mean(mixed * mixed, axis=1, keepdims=True)
-    scaled = (mixed * gain_ref[...]).astype(jnp.bfloat16)
-    out_ref[...] = dot(scaled, label_ref[...]) / jnp.sqrt(mean_sq + 1e-05)
+    own, width = tok_ref.shape
+    half = width // 2
+    square = jnp.zeros((own, 1), jnp.float32)
+    product = jnp.zeros(out_ref.shape, jnp.float32)
+    for side in range(2):
+        cols = slice(side * half, (side + 1) * half)
+        mixed = tok_ref[:, cols].astype(jnp.float32)
+        for ref in refs[3 * side : 3 * side + 3]:
+            mixed = mixed + ref[:own].astype(jnp.float32)
+        square = square + jnp.sum(mixed * mixed, axis=1, keepdims=True)
+        scaled = (mixed * gain_ref[:, cols]).astype(jnp.bfloat16)
+        product = product + dot(scaled, label_ref[cols])
+    out_ref[...] = product / jnp.sqrt(square / width + 1e-05)
 
 
 def body(tokens, w_qkv, w_out, norm_gain, w_label, offset_mid, offset_far):
@@ -296,11 +308,12 @@
 
     own = rows // head_count
     place_arr = place.astype(jnp.int32).reshape(1)
-    parts = pl.pallas_call(
+    half = width // 2
+    kept_a, sent_a, kept_b, sent_b = pl.pallas_call(
         functools.partial(wide_kernel, *sizes, head_count),
         in_specs=[HBM, HBM, SMEM] + [VMEM] * 7 + [HBM],
-        out_specs=[VMEM] * head_count,
-        out_shape=[bf16(own, width)] * head_count,
+        out_specs=[VMEM] * 4,
+        out_shape=[bf16(2 * own, half)] * 4,
         scratch_shapes=[
             pltpu.VMEM((rows, cols), jnp.float32),
             *off_scratch,
@@ -314,10 +327,12 @@
         mid_line, mid_other, far_line, far_other, w_out,
     )
 
-    got = [parts[0]]
-    for step in range(1, head_count):
-        route = [(i, i ^ step) for i in range(head_count)]
-        got.append(lax.ppermute(parts[step], "head", route))
+    swap = lambda a, step: lax.ppermute(a, "head", [(i, i ^ step) for i in range(head_count)])
+    got_a, got_b = swap(sent_a, 1), swap(sent_b, 3)
+    tail = lambda a: a[own:].astype(jnp.float32)
+    last_a = swap((tail(kept_a) + tail(got_a)).astype(jnp.bfloat16), 3)
+    last_b = swap((tail(kept_b) + tail(got_b)).astype(jnp.bfloat16), 1)
+    got = [kept_a, got_a, last_a, kept_b, got_b, last_b]
 
     whole = lambda *shape: pl.BlockSpec(shape, lambda i, p: (0,) * len(shape))
     logit = pl.pallas_call(
@@ -330,7 +345,7 @@
                 whole(1, width),
                 whole(*w_label.shape),
             ]
-            + [whole(own, width)] * head_count,
+            + [whole(own, half)] * len(got),
             out_specs=whole(own, w_label.shape[1]),
         ),
         out_shape=jax.ShapeDtypeStruct((own, w_label.shape[1]), jnp.float32),

time: 65.8 us -> 64.3 us (0.977); the launches traced: 64.7 us -> 64.1 us
  waiting for transfers between devices: 22.4 us -> 21.3 us
    ppermute x3 -> x4, waiting for transfers between devices: 14.1 us -> 12 us  [body(): lax.ppermute(a, 'head', [(i, i ^ step) for i in range(head_count)])]
    ppermute x6, waiting for transfers between devices: 6.84 us -> 7.96 us  [share(): pieces.append(lax.ppermute(block, axis, route))]
    ppermute x3 -> x4, starting transfers between devices: 4.79 us -> 5.16 us  [body(): lax.ppermute(a, 'head', [(i, i ^ step) for i in range(head_count)])]
  transfers between devices with their start and end apart: 12 -> 13, of which waited for: 9 -> 9; matrix products, arithmetic and copies ran while one was open for 0% -> 0% of each run, Pallas kernels for 5% -> 6%
where the time goes in v4:
time: 64.3 us; the launch traced here: 64.1 us
  starting transfers between devices  29.7 us (46%)
  waiting for transfers between devices  21.3 us (33%)
  Pallas kernels  12.1 us (19%)
  local copies, waits for them, and re-layouts  0.7 us (1%)
    ppermute x6, starting transfers between devices, share(): pieces.append(lax.ppermute(block, axis, route))  12.6 us
    ppermute x4, waiting for transfers between devices, body(): lax.ppermute(a, 'head', [(i, i ^ step) for i in range(head_count)])  12 us
    all_to_all x1, starting transfers between devices, body(): far_line = lax.all_to_all(far_kv, 'seq', 0, 0, axis_index_groups=chips)  11.4 us
    ppermute x6, waiting for transfers between devices, share(): pieces.append(lax.ppermute(block, axis, route))  7.96 us
    ppermute x4, starting transfers between devices, body(): lax.ppermute(a, 'head', [(i, i ^ step) for i in range(head_count)])  5.16 us
    pallas_call x1, Pallas kernels, body(): pl.pallas_call(functools.partial(kv_kernel, *sizes), in_specs=[HBM] * 4,...  4.19 us
    pallas_call x1, Pallas kernels, body(): pl.pallas_call(functools.partial(near_kernel, *sizes), in_specs=[HBM] * 4...  3.58 us
    pallas_call x1, Pallas kernels, body(): pl.pallas_call(functools.partial(wide_kernel, *sizes, head_count), in_spe...  3.1 us
  transfers between devices with their start and end apart: 13, of which 9 were waited for; matrix products, arithmetic and copies ran while one was open for 0% of the time, Pallas kernels for 6%

profile of v4, /device:TPU:32, one launch (start us, length us, event | category | flops | bytes accessed | tf_op | source)
XLA Modules:
  0.0 64.1 jit_solution(9201326352088473105)
XLA Ops:
  0.0 4.2 %keys_values.1 = (bf16[2,256,512]{2,1,0:T(8,128)(2,1)S(1)}, bf16[1,2,4,32,128]{4,3,2,1,0:T(8,128)(2,1)S(1)}, bf16[32,2,16,128]{3,2,1,0:T(8,128)(2,1)}) custom-call(s32[4]{0:T(128)} %mid_hbm.5, s32[4]{0:T(128)} %far_hbm.5, bf16[256,2048]{1,0:T(8,128)(2,1)} %tok_ref.1, bf16[3,2048,512]{2,1,0:T(8,128)(2,1)} %bitcast.21), custom_call_target="tpu_custom_call" | custom-call | tf_op jit(solution)/shard_map/keys_values/pallas_call | solution.py:267
  4.2 11.4 %all-to-all-start = ((bf16[32,2,16,128]{3,2,1,0:T(8,128)(2,1)}), bf16[32,2,16,128]{3,2,1,0:T(8,128)(2,1)S(1)}, u32[]{:S(2)}, u32[]{:S(2)}) async-start(bf16[32,2,16,128]{3,2,1,0:T(8,128)(2,1)} %get-tuple-element.28), calls=%async_computation | async-start | bytes 524288 | tf_op jit(solution)/shard_map/all_to_all | solution.py:287
  15.6 0.3 collective-permute-start
  15.9 6.1 %collective-permute-start.1 = (bf16[2,4,32,128]{3,2,1,0:T(8,128)(2,1)S(1)}, bf16[2,4,32,128]{3,2,1,0:T(8,128)(2,1)S(1)}, u32[]{:S(2)}, u32[]{:S(2)}) collective-permute-start(bf16[2,4,32,128]{3,2,1,0:T(8,128)(2,1)S(1)} %bitcast.18), channel_id=1, source_target_pairs={{240,0},{248,8},{0,240},{8,248},{244,4},{252,12},{4,244},{12,252},... | collective-permute-start | bytes 196616 | tf_op jit(solution)/shard_map/ppermute | solution.py:34
  22.0 1.4 %collective-permute-start.2 = (bf16[2,4,32,128]{3,2,1,0:T(8,128)(2,1)S(1)}, bf16[2,4,32,128]{3,2,1,0:T(8,128)(2,1)S(1)}, u32[]{:S(2)}, u32[]{:S(2)}) collective-permute-start(bf16[2,4,32,128]{3,2,1,0:T(8,128)(2,1)S(1)} %bitcast.19), channel_id=1, source_target_pairs={{240,8},{248,0},{0,248},{8,240},{244,12},{252,4},{4,252},{12,244},... | collective-permute-start | bytes 196616 | tf_op jit(solution)/shard_map/ppermute | solution.py:34
  23.4 3.6 %near.1 = (bf16[256,512]{1,0:T(8,128)(2,1)S(1)}, bf16[4,40,128]{2,1,0:T(8,128)(2,1)S(1)}) custom-call(s32[4]{0:T(128)} %mid_hbm.5, s32[4]{0:T(128)} %far_hbm.5, bf16[256,2048]{1,0:T(8,128)(2,1)} %tok_ref.1, bf16[3,2048,512]{2,1,0:T(8,128)(2,1)} %bitcast.22, bf16[2,256,512]{2,1,0:T(8,128)(2,1)S(1)} %get-tuple-element.19.kv_ref), custom_call_target="tpu_custom_call" | custom-call | tf_op jit(solution)/shard_map/near/pallas_call | solution.py:289
  27.0 4.5 %collective-permute-done.2 = bf16[2,4,32,128]{3,2,1,0:T(8,128)(2,1)S(1)} collective-permute-done((bf16[2,4,32,128]{3,2,1,0:T(8,128)(2,1)S(1)}, bf16[2,4,32,128]{3,2,1,0:T(8,128)(2,1)S(1)}, u32[]{:S(2)}, u32[]{:S(2)}) %collective-permute-start.2) | collective-permute-done | bytes 65568 | tf_op jit(solution)/shard_map/ppermute | solution.py:34
  31.6 0.5 collective-permute-start.4
  32.1 1.0 %collective-permute-done.3.refs_1_ = bf16[4,2,4,32,128]{4,3,2,1,0:T(8,128)(2,1)S(1)} collective-permute-done((bf16[4,2,4,32,128]{4,3,2,1,0:T(8,128)(2,1)S(1)}, bf16[4,2,4,32,128]{4,3,2,1,0:T(8,128)(2,1)S(1)}, u32[]{:S(2)}, u32[]{:S(2)}) %collective-permute-start.3) | collective-permute-done | bytes 262176 | tf_op jit(solution)/shard_map/ppermute | solution.py:306
  33.1 0.4 collective-permute-done.4.refs_3_
  33.5 3.1 %wide.1 = (bf16[128,1024]{1,0:T(8,128)(2,1)S(1)}, bf16[128,1024]{1,0:T(8,128)(2,1)S(1)}, bf16[128,1024]{1,0:T(8,128)(2,1)S(1)}, bf16[128,1024]{1,0:T(8,128)(2,1)S(1)}) custom-call(s32[4]{0:T(128)} %mid_hbm.5, s32[4]{0:T(128)} %far_hbm.5, s32[1]{0:T(128)} %bitcast.place_ref, bf16[4,40,128]{2,1,0:T(8,128)(2,1)S(1)} %get-tuple-element.20.sel_ref, ...), custom_call_target="tpu_custom_call" | custom-call | tf_op jit(solution)/shard_map/wide/pallas_call | solution.py:312
  36.6 2.8 %collective-permute-start.7 = (bf16[128,1024]{1,0:T(8,128)(2,1)S(1)}, bf16[128,1024]{1,0:T(8,128)(2,1)S(1)}, u32[]{:S(2)}, u32[]{:S(2)}) collective-permute-start(bf16[128,1024]{1,0:T(8,128)(2,1)S(1)} %get-tuple-element.32), channel_id=1, source_target_pairs={{0,3},{1,2},{2,1},{3,0},{4,7},{5,6},{6,5},{7,4},{8,11},{9,10},{10,... | collective-permute-start | bytes 786440 | tf_op jit(solution)/shard_map/ppermute | solution.py:330
  39.7 6.6 %collective-permute-done.7.refs_4_ = bf16[128,1024]{1,0:T(8,128)(2,1)S(1)} collective-permute-done((bf16[128,1024]{1,0:T(8,128)(2,1)S(1)}, bf16[128,1024]{1,0:T(8,128)(2,1)S(1)}, u32[]{:S(2)}, u32[]{:S(2)}) %collective-permute-start.7) | collective-permute-done | bytes 262176 | tf_op jit(solution)/shard_map/ppermute | solution.py:330
  46.3 0.4 collective-permute-start.8
  46.7 0.9 %collective-permute-done.5.refs_1_ = bf16[128,1024]{1,0:T(8,128)(2,1)S(1)} collective-permute-done((bf16[128,1024]{1,0:T(8,128)(2,1)S(1)}, bf16[128,1024]{1,0:T(8,128)(2,1)S(1)}, u32[]{:S(2)}, u32[]{:S(2)}) %collective-permute-start.5) | collective-permute-done | bytes 262176 | tf_op jit(solution)/shard_map/ppermute | solution.py:330
  47.6 1.7 %collective-permute-start.6 = (bf16[64,1024]{1,0:T(8,128)(2,1)S(1)}, bf16[64,1024]{1,0:T(8,128)(2,1)S(1)}, u32[]{:S(2)}, u32[]{:S(2)}) collective-permute-start(bf16[64,1024]{1,0:T(8,128)(2,1)S(1)} %add_convert_fusion.1), channel_id=1, source_target_pairs={{0,3},{1,2},{2,1},{3,0},{4,7},{5,6},{6,5},{7,4},{8,11},{9,10},{10,... | collective-permute-start | bytes 393224 | tf_op jit(solution)/shard_map/ppermute | solution.py:330
  49.3 2.1 %collective-permute-done.8.refs_5_ = bf16[64,1024]{1,0:T(8,128)(2,1)S(1)} collective-permute-done((bf16[64,1024]{1,0:T(8,128)(2,1)S(1)}, bf16[64,1024]{1,0:T(8,128)(2,1)S(1)}, u32[]{:S(2)}, u32[]{:S(2)}) %collective-permute-start.8) | collective-permute-done | bytes 131104 | tf_op jit(solution)/shard_map/ppermute | solution.py:330
  51.4 2.5 %collective-permute-done.6.refs_2_ = bf16[64,1024]{1,0:T(8,128)(2,1)S(1)} collective-permute-done((bf16[64,1024]{1,0:T(8,128)(2,1)S(1)}, bf16[64,1024]{1,0:T(8,128)(2,1)S(1)}, u32[]{:S(2)}, u32[]{:S(2)}) %collective-permute-start.6) | collective-permute-done | bytes 131104 | tf_op jit(solution)/shard_map/ppermute | solution.py:330
  53.8 1.2 %logits.1 = f32[64,128]{1,0:T(8,128)S(1)} custom-call(s32[1]{0:T(128)} %bitcast.place_ref, bf16[256,2048]{1,0:T(8,128)(2,1)} %tok_ref.1, f32[1,2048]{1,0:T(1,128)S(1)} %bitcast.20, bf16[2048,128]{1,0:T(8,128)(2,1)S(1)} %copy-done, bf16[128,1024]{1,0:T(8,128)(2,1)S(1)} %get-tuple-element.29.refs_0_, bf16[128,1024]{1,0:T(8,128)(2,1)S(1)} %collective-permute-done.5.refs_1_, ...), custom_call_target="tpu_custom_call" | custom-call | tf_op jit(solution)/shard_map/logits/pallas_call | solution.py:338
  55.2 3.1 %collective-permute-start.10 = (f32[64,128]{1,0:T(8,128)S(1)}, f32[64,128]{1,0:T(8,128)S(1)}, u32[]{:S(2)}, u32[]{:S(2)}) collective-permute-start(f32[64,128]{1,0:T(8,128)S(1)} %logits.1), channel_id=1, source_target_pairs={{0,2},{1,3},{2,0},{3,1},{4,6},{5,7},{6,4},{7,5},{8,10},{9,11},{10,... | collective-permute-start | bytes 98312 | tf_op jit(solution)/shard_map/ppermute | solution.py:34
  58.3 1.6 %collective-permute-start.11 = (f32[64,128]{1,0:T(8,128)S(1)}, f32[64,128]{1,0:T(8,128)S(1)}, u32[]{:S(2)}, u32[]{:S(2)}) collective-permute-start(f32[64,128]{1,0:T(8,128)S(1)} %logits.1), channel_id=1, source_target_pairs={{0,3},{1,2},{2,1},{3,0},{4,7},{5,6},{6,5},{7,4},{8,11},{9,10},{10,... | collective-permute-start | bytes 98312 | tf_op jit(solution)/shard_map/ppermute | solution.py:34
  59.9 0.8 %collective-permute-done.10 = f32[64,128]{1,0:T(8,128)S(1)} collective-permute-done((f32[64,128]{1,0:T(8,128)S(1)}, f32[64,128]{1,0:T(8,128)S(1)}, u32[]{:S(2)}, u32[]{:S(2)}) %collective-permute-start.10) | collective-permute-done | bytes 32800 | tf_op jit(solution)/shard_map/ppermute | solution.py:34
  60.7 2.7 %collective-permute-done.11 = f32[64,128]{1,0:T(8,128)S(1)} collective-permute-done((f32[64,128]{1,0:T(8,128)S(1)}, f32[64,128]{1,0:T(8,128)S(1)}, u32[]{:S(2)}, u32[]{:S(2)}) %collective-permute-start.11) | collective-permute-done | bytes 32800 | tf_op jit(solution)/shard_map/ppermute | solution.py:34
  63.4 0.7 %copy-done.2 = f32[4,64,128]{2,1,0:T(8,128)} copy-done((f32[4,64,128]{2,1,0:T(8,128)}, f32[4,64,128]{2,1,0:T(8,128)S(1)}, u32[]{:S(2)}) %copy-start.2) | copy-done | bytes 131096
  (20 shorter events, 0.6 us)
Async XLA Ops:
  4.2 27.4 %all-to-all-start = ((bf16[32,2,16,128]{3,2,1,0:T(8,128)(2,1)}), bf16[32,2,16,128]{3,2,1,0:T(8,128)(2,1)S(1)}, u32[]{:S(2)}, u32[]{:S(2)}) async-start(bf16[32,2,16,128]{3,2,1,0:T(8,128)(2,1)} %get-tuple-element.28), calls=%async_computation | async-start | bytes 524288 | tf_op jit(solution)/shard_map/all_to_all | solution.py:287
  15.6 11.4 %collective-permute-start = (bf16[2,4,32,128]{3,2,1,0:T(8,128)(2,1)S(1)}, bf16[2,4,32,128]{3,2,1,0:T(8,128)(2,1)S(1)}, u32[]{:S(2)}, u32[]{:S(2)}) collective-permute-start(bf16[2,4,32,128]{3,2,1,0:T(8,128)(2,1)S(1)} %bitcast.17), channel_id=1, source_target_pairs={{240,248},{248,240},{0,8},{8,0},{244,252},{252,244},{4,12},{12,4},... | collective-permute-start | bytes 196616 | tf_op jit(solution)/shard_map/ppermute | solution.py:34
  15.9 11.1 %collective-permute-start.1 = (bf16[2,4,32,128]{3,2,1,0:T(8,128)(2,1)S(1)}, bf16[2,4,32,128]{3,2,1,0:T(8,128)(2,1)S(1)}, u32[]{:S(2)}, u32[]{:S(2)}) collective-permute-start(bf16[2,4,32,128]{3,2,1,0:T(8,128)(2,1)S(1)} %bitcast.18), channel_id=1, source_target_pairs={{240,0},{248,8},{0,240},{8,248},{244,4},{252,12},{4,244},{12,252},... | collective-permute-start | bytes 196616 | tf_op jit(solution)/shard_map/ppermute | solution.py:34
  22.0 9.5 %collective-permute-start.2 = (bf16[2,4,32,128]{3,2,1,0:T(8,128)(2,1)S(1)}, bf16[2,4,32,128]{3,2,1,0:T(8,128)(2,1)S(1)}, u32[]{:S(2)}, u32[]{:S(2)}) collective-permute-start(bf16[2,4,32,128]{3,2,1,0:T(8,128)(2,1)S(1)} %bitcast.19), channel_id=1, source_target_pairs={{240,8},{248,0},{0,248},{8,240},{244,12},{252,4},{4,252},{12,244},... | collective-permute-start | bytes 196616 | tf_op jit(solution)/shard_map/ppermute | solution.py:34
  23.4 30.5 %copy-start = (bf16[2048,128]{1,0:T(8,128)(2,1)S(1)}, bf16[2048,128]{1,0:T(8,128)(2,1)}, u32[]{:S(2)}) copy-start(bf16[2048,128]{1,0:T(8,128)(2,1)} %label_ref.1) | copy-start | bytes 1572868
  23.4 30.5 %copy-start.1 = (f32[2048]{0:T(1024)S(1)}, f32[2048]{0:T(1024)}, u32[]{:S(2)}) copy-start(f32[2048]{0:T(1024)} %param.10) | copy-start | bytes 24580
  31.5 1.6 %collective-permute-start.3 = (bf16[4,2,4,32,128]{4,3,2,1,0:T(8,128)(2,1)S(1)}, bf16[4,2,4,32,128]{4,3,2,1,0:T(8,128)(2,1)S(1)}, u32[]{:S(2)}, u32[]{:S(2)}) collective-permute-start(bf16[4,2,4,32,128]{4,3,2,1,0:T(8,128)(2,1)S(1)} %pad_maximum_fusion.refs_0_), channel_id=1, source_target_pairs={{0,4},{4,0},{8,12},{12,8},{16,20},{20,16},{24,28},{28,24},{32,36},... | collective-permute-start | bytes 786440 | tf_op jit(solution)/shard_map/ppermute | solution.py:306
  31.6 1.9 %collective-permute-start.4 = (bf16[32,2,16,128]{3,2,1,0:T(8,128)(2,1)S(1)}, bf16[32,2,16,128]{3,2,1,0:T(8,128)(2,1)S(1)}, u32[]{:S(2)}, u32[]{:S(2)}) collective-permute-start(bf16[32,2,16,128]{3,2,1,0:T(8,128)(2,1)S(1)} %all-to-all-done.refs_2_), channel_id=1, source_target_pairs={{0,4},{4,0},{8,12},{12,8},{16,20},{20,16},{24,28},{28,24},{32,36},... | collective-permute-start | bytes 786440 | tf_op jit(solution)/shard_map/ppermute | solution.py:307
  36.6 9.6 %collective-permute-start.7 = (bf16[128,1024]{1,0:T(8,128)(2,1)S(1)}, bf16[128,1024]{1,0:T(8,128)(2,1)S(1)}, u32[]{:S(2)}, u32[]{:S(2)}) collective-permute-start(bf16[128,1024]{1,0:T(8,128)(2,1)S(1)} %get-tuple-element.32), channel_id=1, source_target_pairs={{0,3},{1,2},{2,1},{3,0},{4,7},{5,6},{6,5},{7,4},{8,11},{9,10},{10,... | collective-permute-start | bytes 786440 | tf_op jit(solution)/shard_map/ppermute | solution.py:330
  39.5 8.1 %collective-permute-start.5 = (bf16[128,1024]{1,0:T(8,128)(2,1)S(1)}, bf16[128,1024]{1,0:T(8,128)(2,1)S(1)}, u32[]{:S(2)}, u32[]{:S(2)}) collective-permute-start(bf16[128,1024]{1,0:T(8,128)(2,1)S(1)} %get-tuple-element.30), channel_id=1, source_target_pairs={{0,1},{1,0},{2,3},{3,2},{4,5},{5,4},{6,7},{7,6},{8,9},{9,8},{10,11... | collective-permute-start | bytes 786440 | tf_op jit(solution)/shard_map/ppermute | solution.py:330
  46.3 5.1 %collective-permute-start.8 = (bf16[64,1024]{1,0:T(8,128)(2,1)S(1)}, bf16[64,1024]{1,0:T(8,128)(2,1)S(1)}, u32[]{:S(2)}, u32[]{:S(2)}) collective-permute-start(bf16[64,1024]{1,0:T(8,128)(2,1)S(1)} %add_convert_fusion), channel_id=1, source_target_pairs={{0,1},{1,0},{2,3},{3,2},{4,5},{5,4},{6,7},{7,6},{8,9},{9,8},{10,11... | collective-permute-start | bytes 393224 | tf_op jit(solution)/shard_map/ppermute | solution.py:330
  47.6 6.3 %collective-permute-start.6 = (bf16[64,1024]{1,0:T(8,128)(2,1)S(1)}, bf16[64,1024]{1,0:T(8,128)(2,1)S(1)}, u32[]{:S(2)}, u32[]{:S(2)}) collective-permute-start(bf16[64,1024]{1,0:T(8,128)(2,1)S(1)} %add_convert_fusion.1), channel_id=1, source_target_pairs={{0,3},{1,2},{2,1},{3,0},{4,7},{5,6},{6,5},{7,4},{8,11},{9,10},{10,... | collective-permute-start | bytes 393224 | tf_op jit(solution)/shard_map/ppermute | solution.py:330
  55.1 4.8 %collective-permute-start.9 = (f32[64,128]{1,0:T(8,128)S(1)}, f32[64,128]{1,0:T(8,128)S(1)}, u32[]{:S(2)}, u32[]{:S(2)}) collective-permute-start(f32[64,128]{1,0:T(8,128)S(1)} %logits.1), channel_id=1, source_target_pairs={{0,1},{1,0},{2,3},{3,2},{4,5},{5,4},{6,7},{7,6},{8,9},{9,8},{10,11... | collective-permute-start | bytes 98312 | tf_op jit(solution)/shard_map/ppermute | solution.py:34
  55.2 5.5 %collective-permute-start.10 = (f32[64,128]{1,0:T(8,128)S(1)}, f32[64,128]{1,0:T(8,128)S(1)}, u32[]{:S(2)}, u32[]{:S(2)}) collective-permute-start(f32[64,128]{1,0:T(8,128)S(1)} %logits.1), channel_id=1, source_target_pairs={{0,2},{1,3},{2,0},{3,1},{4,6},{5,7},{6,4},{7,5},{8,10},{9,11},{10,... | collective-permute-start | bytes 98312 | tf_op jit(solution)/shard_map/ppermute | solution.py:34
  58.3 5.1 %collective-permute-start.11 = (f32[64,128]{1,0:T(8,128)S(1)}, f32[64,128]{1,0:T(8,128)S(1)}, u32[]{:S(2)}, u32[]{:S(2)}) collective-permute-start(f32[64,128]{1,0:T(8,128)S(1)} %logits.1), channel_id=1, source_target_pairs={{0,3},{1,2},{2,1},{3,0},{4,7},{5,6},{6,5},{7,4},{8,11},{9,10},{10,... | collective-permute-start | bytes 98312 | tf_op jit(solution)/shard_map/ppermute | solution.py:34
  63.4 0.7 %copy-start.2 = (f32[4,64,128]{2,1,0:T(8,128)}, f32[4,64,128]{2,1,0:T(8,128)S(1)}, u32[]{:S(2)}) copy-start(f32[4,64,128]{2,1,0:T(8,128)S(1)} %bitcast_dynamic-update-slice_fusion) | copy-start | bytes 393220

commit v5 on v4

--- a/solution.py
+++ b/solution.py
@@ -119,11 +119,15 @@
             far_out[j, c] = few
 
 
-def near_kernel(rows, heads, size, seq_count, mid_hbm, far_hbm, tok_hbm, w_hbm, kv_ref,
-                near_ref, sel_ref, tok_ref, w_ref, mid_ref, far_ref, off_sems, sems):
+def near_kernel(rows, heads, size, seq_count, mid_hbm, far_hbm, place_ref, tok_hbm, w_hbm, kv_ref,
+                near_ref, sel_ref, own_ref, tok_ref, w_ref, mid_ref, far_ref, off_sems, sems):
     offsets = offset_copies(mid_hbm, far_hbm, mid_ref, far_ref, off_sems)
     product = load_and_project((0,), tok_hbm, w_hbm, tok_ref, w_ref, sems)
     whole = product(0)
+    own, deep = own_ref.shape[0], tok_ref.shape[2]
+    mine = pl.ds(pl.multiple_of(place_ref[0] * own, own), own)
+    for k in range(tok_ref.shape[0]):
+        own_ref[:, k * deep : (k + 1) * deep] = tok_ref[k, mine, :]
     for copy in offsets:
         copy.wait()
     for h in range(heads):
@@ -217,7 +221,7 @@
                 outs[2 * side + name][i * own : (i + 1) * own, to] = part[s * own : (s + 1) * own]
 
 
-def logits_kernel(place_ref, tok_ref, gain_ref, label_ref, *refs):
+def logits_kernel(tok_ref, gain_ref, label_ref, *refs):
     out_ref = refs[-1]
     own, width = tok_ref.shape
     half = width // 2
@@ -286,11 +290,13 @@
 
     far_line = lax.all_to_all(far_kv, "seq", 0, 0, axis_index_groups=chips)
     mid_pieces = share(mid_kv[0], "seq", across)
-    near, sel = pl.pallas_call(
+    own = rows // head_count
+    place_arr = place.astype(jnp.int32).reshape(1)
+    near, sel, own_tokens = pl.pallas_call(
         functools.partial(near_kernel, *sizes),
-        in_specs=[HBM] * 4 + [VMEM],
-        out_specs=[VMEM] * 2,
-        out_shape=[bf16(rows, cols), bf16(heads, PICKS, size)],
+        in_specs=[HBM, HBM, SMEM, HBM, HBM, VMEM],
+        out_specs=[VMEM] * 3,
+        out_shape=[bf16(rows, cols), bf16(heads, PICKS, size), bf16(own, width)],
         scratch_shapes=[
             tok_scratch,
             pltpu.VMEM((1, steps, deep, cols), jnp.bfloat16),
@@ -299,15 +305,13 @@
         ],
         compiler_params=params(14),
         name="near",
-    )(offset_mid, offset_far, tokens, weights, kv)
+    )(offset_mid, offset_far, place_arr, tokens, weights, kv)
 
     *mid_pieces, near = lax.optimization_barrier((*mid_pieces, near))
     mid_line = jnp.stack(mid_pieces)
     mid_other = lax.ppermute(mid_line, "seq", cores)
     far_other = lax.ppermute(far_line, "seq", cores)
 
-    own = rows // head_count
-    place_arr = place.astype(jnp.int32).reshape(1)
     half = width // 2
     kept_a, sent_a, kept_b, sent_b = pl.pallas_call(
         functools.partial(wide_kernel, *sizes, head_count),
@@ -334,24 +338,14 @@
     last_b = swap((tail(kept_b) + tail(got_b)).astype(jnp.bfloat16), 1)
     got = [kept_a, got_a, last_a, kept_b, got_b, last_b]
 
-    whole = lambda *shape: pl.BlockSpec(shape, lambda i, p: (0,) * len(shape))
     logit = pl.pallas_call(
         logits_kernel,
-        grid_spec=pltpu.PrefetchScalarGridSpec(
-            num_scalar_prefetch=1,
-            grid=(1,),
-            in_specs=[
-                pl.BlockSpec((own, width), lambda i, p: (p[0], 0)),
-                whole(1, width),
-                whole(*w_label.shape),
-            ]
-            + [whole(own, half)] * len(got),
-            out_specs=whole(own, w_label.shape[1]),
-        ),
+        in_specs=[VMEM] * (3 + len(got)),
+        out_specs=VMEM,
         out_shape=jax.ShapeDtypeStruct((own, w_label.shape[1]), jnp.float32),
         compiler_params=params(10),
         name="logits",
-    )(place_arr, tokens, norm_gain.reshape(1, width), w_label, *got)
+    )(own_tokens, norm_gain.reshape(1, width), w_label, *got)
 
     every = share(logit, "head", [list(range(head_count))])
     logits = jnp.zeros((head_count,) + logit.shape, jnp.float32)

time: 64.3 us -> 63.3 us (0.984)
  Pallas kernels: 12.1 us -> 11.2 us
    pallas_call x2, Pallas kernels: 4.82 us -> 3.89 us  [the longest x1 3.6 us: body(): pl.pallas_call(functools.partial(near_kernel, *sizes), in_specs=[HBM, HBM...]
where the time goes in v5:
time: 63.3 us; the launch traced here: 63.1 us
  starting transfers between devices  29.7 us (47%)
  waiting for transfers between devices  21.3 us (34%)
  Pallas kernels  11.2 us (18%)
  local copies, waits for them, and re-layouts  0.7 us (1%)
    ppermute x6, starting transfers between devices, share(): pieces.append(lax.ppermute(block, axis, route))  12.6 us
    ppermute x4, waiting for transfers between devices, body(): lax.ppermute(a, 'head', [(i, i ^ step) for i in range(head_count)])  12 us
    all_to_all x1, starting transfers between devices, body(): far_line = lax.all_to_all(far_kv, 'seq', 0, 0, axis_index_groups=chips)  11.4 us
    ppermute x6, waiting for transfers between devices, share(): pieces.append(lax.ppermute(block, axis, route))  7.95 us
    ppermute x4, starting transfers between devices, body(): lax.ppermute(a, 'head', [(i, i ^ step) for i in range(head_count)])  5.16 us
    pallas_call x1, Pallas kernels, body(): pl.pallas_call(functools.partial(kv_kernel, *sizes), in_specs=[HBM] * 4,...  4.19 us
    pallas_call x1, Pallas kernels, body(): pl.pallas_call(functools.partial(near_kernel, *sizes), in_specs=[HBM, HBM...  3.6 us
    pallas_call x1, Pallas kernels, body(): pl.pallas_call(functools.partial(wide_kernel, *sizes, head_count), in_spe...  3.1 us
  transfers between devices with their start and end apart: 13, of which 9 were waited for; matrix products, arithmetic and copies ran while one was open for 0% of the time, Pallas kernels for 6%

profile of v5, /device:TPU:32, one launch (start us, length us, event | category | flops | bytes accessed | tf_op | source)
XLA Modules:
  0.0 63.1 jit_solution(4879335362423538092)
XLA Ops:
  0.0 4.2 %keys_values.1 = (bf16[2,256,512]{2,1,0:T(8,128)(2,1)S(1)}, bf16[1,2,4,32,128]{4,3,2,1,0:T(8,128)(2,1)S(1)}, bf16[32,2,16,128]{3,2,1,0:T(8,128)(2,1)}) custom-call(s32[4]{0:T(128)} %mid_hbm.5, s32[4]{0:T(128)} %far_hbm.5, bf16[256,2048]{1,0:T(8,128)(2,1)} %tok_hbm.3, bf16[3,2048,512]{2,1,0:T(8,128)(2,1)} %bitcast.21), custom_call_target="tpu_custom_call" | custom-call | tf_op jit(solution)/shard_map/keys_values/pallas_call | solution.py:271
  4.2 11.4 %all-to-all-start = ((bf16[32,2,16,128]{3,2,1,0:T(8,128)(2,1)}), bf16[32,2,16,128]{3,2,1,0:T(8,128)(2,1)S(1)}, u32[]{:S(2)}, u32[]{:S(2)}) async-start(bf16[32,2,16,128]{3,2,1,0:T(8,128)(2,1)} %get-tuple-element.30), calls=%async_computation | async-start | bytes 524288 | tf_op jit(solution)/shard_map/all_to_all | solution.py:291
  15.6 0.3 collective-permute-start
  15.9 6.1 %collective-permute-start.1 = (bf16[2,4,32,128]{3,2,1,0:T(8,128)(2,1)S(1)}, bf16[2,4,32,128]{3,2,1,0:T(8,128)(2,1)S(1)}, u32[]{:S(2)}, u32[]{:S(2)}) collective-permute-start(bf16[2,4,32,128]{3,2,1,0:T(8,128)(2,1)S(1)} %bitcast.18), channel_id=1, source_target_pairs={{240,0},{248,8},{0,240},{8,248},{244,4},{252,12},{4,244},{12,252},... | collective-permute-start | bytes 196616 | tf_op jit(solution)/shard_map/ppermute | solution.py:34
  22.0 1.4 %collective-permute-start.2 = (bf16[2,4,32,128]{3,2,1,0:T(8,128)(2,1)S(1)}, bf16[2,4,32,128]{3,2,1,0:T(8,128)(2,1)S(1)}, u32[]{:S(2)}, u32[]{:S(2)}) collective-permute-start(bf16[2,4,32,128]{3,2,1,0:T(8,128)(2,1)S(1)} %bitcast.19), channel_id=1, source_target_pairs={{240,8},{248,0},{0,248},{8,240},{244,12},{252,4},{4,252},{12,244},... | collective-permute-start | bytes 196616 | tf_op jit(solution)/shard_map/ppermute | solution.py:34
  23.4 3.6 %near.1 = (bf16[256,512]{1,0:T(8,128)(2,1)S(1)}, bf16[4,40,128]{2,1,0:T(8,128)(2,1)S(1)}, bf16[64,2048]{1,0:T(8,128)(2,1)S(1)}) custom-call(s32[4]{0:T(128)} %mid_hbm.5, s32[4]{0:T(128)} %far_hbm.5, s32[1]{0:T(128)} %bitcast.place_ref, bf16[256,2048]{1,0:T(8,128)(2,1)} %tok_hbm.3, bf16[3,2048,512]{2,1,0:T(8,128)(2,1)} %bitcast.22, ...), custom_call_target="tpu_custom_call" | custom-call | tf_op jit(solution)/shard_map/near/pallas_call | solution.py:295
  27.0 4.5 %collective-permute-done.2 = bf16[2,4,32,128]{3,2,1,0:T(8,128)(2,1)S(1)} collective-permute-done((bf16[2,4,32,128]{3,2,1,0:T(8,128)(2,1)S(1)}, bf16[2,4,32,128]{3,2,1,0:T(8,128)(2,1)S(1)}, u32[]{:S(2)}, u32[]{:S(2)}) %collective-permute-start.2) | collective-permute-done | bytes 65568 | tf_op jit(solution)/shard_map/ppermute | solution.py:34
  31.6 0.5 collective-permute-start.4
  32.1 1.0 %collective-permute-done.3.refs_1_ = bf16[4,2,4,32,128]{4,3,2,1,0:T(8,128)(2,1)S(1)} collective-permute-done((bf16[4,2,4,32,128]{4,3,2,1,0:T(8,128)(2,1)S(1)}, bf16[4,2,4,32,128]{4,3,2,1,0:T(8,128)(2,1)S(1)}, u32[]{:S(2)}, u32[]{:S(2)}) %collective-permute-start.3) | collective-permute-done | bytes 262176 | tf_op jit(solution)/shard_map/ppermute | solution.py:312
  33.1 0.4 collective-permute-done.4.refs_3_
  33.5 3.1 %wide.1 = (bf16[128,1024]{1,0:T(8,128)(2,1)S(1)}, bf16[128,1024]{1,0:T(8,128)(2,1)S(1)}, bf16[128,1024]{1,0:T(8,128)(2,1)S(1)}, bf16[128,1024]{1,0:T(8,128)(2,1)S(1)}) custom-call(s32[4]{0:T(128)} %mid_hbm.5, s32[4]{0:T(128)} %far_hbm.5, s32[1]{0:T(128)} %bitcast.place_ref, bf16[4,40,128]{2,1,0:T(8,128)(2,1)S(1)} %get-tuple-element.22.sel_ref, ...), custom_call_target="tpu_custom_call" | custom-call | tf_op jit(solution)/shard_map/wide/pallas_call | solution.py:316
  36.6 2.8 %collective-permute-start.7 = (bf16[128,1024]{1,0:T(8,128)(2,1)S(1)}, bf16[128,1024]{1,0:T(8,128)(2,1)S(1)}, u32[]{:S(2)}, u32[]{:S(2)}) collective-permute-start(bf16[128,1024]{1,0:T(8,128)(2,1)S(1)} %get-tuple-element.34), channel_id=1, source_target_pairs={{0,3},{1,2},{2,1},{3,0},{4,7},{5,6},{6,5},{7,4},{8,11},{9,10},{10,... | collective-permute-start | bytes 786440 | tf_op jit(solution)/shard_map/ppermute | solution.py:334
  39.7 6.6 %collective-permute-done.7.refs_4_ = bf16[128,1024]{1,0:T(8,128)(2,1)S(1)} collective-permute-done((bf16[128,1024]{1,0:T(8,128)(2,1)S(1)}, bf16[128,1024]{1,0:T(8,128)(2,1)S(1)}, u32[]{:S(2)}, u32[]{:S(2)}) %collective-permute-start.7) | collective-permute-done | bytes 262176 | tf_op jit(solution)/shard_map/ppermute | solution.py:334
  46.3 0.4 collective-permute-start.8
  46.7 0.9 %collective-permute-done.5.refs_1_ = bf16[128,1024]{1,0:T(8,128)(2,1)S(1)} collective-permute-done((bf16[128,1024]{1,0:T(8,128)(2,1)S(1)}, bf16[128,1024]{1,0:T(8,128)(2,1)S(1)}, u32[]{:S(2)}, u32[]{:S(2)}) %collective-permute-start.5) | collective-permute-done | bytes 262176 | tf_op jit(solution)/shard_map/ppermute | solution.py:334
  47.6 1.7 %collective-permute-start.6 = (bf16[64,1024]{1,0:T(8,128)(2,1)S(1)}, bf16[64,1024]{1,0:T(8,128)(2,1)S(1)}, u32[]{:S(2)}, u32[]{:S(2)}) collective-permute-start(bf16[64,1024]{1,0:T(8,128)(2,1)S(1)} %add_convert_fusion.1), channel_id=1, source_target_pairs={{0,3},{1,2},{2,1},{3,0},{4,7},{5,6},{6,5},{7,4},{8,11},{9,10},{10,... | collective-permute-start | bytes 393224 | tf_op jit(solution)/shard_map/ppermute | solution.py:334
  49.3 2.1 %collective-permute-done.8.refs_5_ = bf16[64,1024]{1,0:T(8,128)(2,1)S(1)} collective-permute-done((bf16[64,1024]{1,0:T(8,128)(2,1)S(1)}, bf16[64,1024]{1,0:T(8,128)(2,1)S(1)}, u32[]{:S(2)}, u32[]{:S(2)}) %collective-permute-start.8) | collective-permute-done | bytes 131104 | tf_op jit(solution)/shard_map/ppermute | solution.py:334
  51.4 2.5 %collective-permute-done.6.refs_2_ = bf16[64,1024]{1,0:T(8,128)(2,1)S(1)} collective-permute-done((bf16[64,1024]{1,0:T(8,128)(2,1)S(1)}, bf16[64,1024]{1,0:T(8,128)(2,1)S(1)}, u32[]{:S(2)}, u32[]{:S(2)}) %collective-permute-start.6) | collective-permute-done | bytes 131104 | tf_op jit(solution)/shard_map/ppermute | solution.py:334
  53.8 0.3 logits.1
  54.2 3.1 %collective-permute-start.10 = (f32[64,128]{1,0:T(8,128)S(1)}, f32[64,128]{1,0:T(8,128)S(1)}, u32[]{:S(2)}, u32[]{:S(2)}) collective-permute-start(f32[64,128]{1,0:T(8,128)S(1)} %logits.1), channel_id=1, source_target_pairs={{0,2},{1,3},{2,0},{3,1},{4,6},{5,7},{6,4},{7,5},{8,10},{9,11},{10,... | collective-permute-start | bytes 98312 | tf_op jit(solution)/shard_map/ppermute | solution.py:34
  57.3 1.6 %collective-permute-start.11 = (f32[64,128]{1,0:T(8,128)S(1)}, f32[64,128]{1,0:T(8,128)S(1)}, u32[]{:S(2)}, u32[]{:S(2)}) collective-permute-start(f32[64,128]{1,0:T(8,128)S(1)} %logits.1), channel_id=1, source_target_pairs={{0,3},{1,2},{2,1},{3,0},{4,7},{5,6},{6,5},{7,4},{8,11},{9,10},{10,... | collective-permute-start | bytes 98312 | tf_op jit(solution)/shard_map/ppermute | solution.py:34
  59.0 0.8 %collective-permute-done.10 = f32[64,128]{1,0:T(8,128)S(1)} collective-permute-done((f32[64,128]{1,0:T(8,128)S(1)}, f32[64,128]{1,0:T(8,128)S(1)}, u32[]{:S(2)}, u32[]{:S(2)}) %collective-permute-start.10) | collective-permute-done | bytes 32800 | tf_op jit(solution)/shard_map/ppermute | solution.py:34
  59.7 2.7 %collective-permute-done.11 = f32[64,128]{1,0:T(8,128)S(1)} collective-permute-done((f32[64,128]{1,0:T(8,128)S(1)}, f32[64,128]{1,0:T(8,128)S(1)}, u32[]{:S(2)}, u32[]{:S(2)}) %collective-permute-start.11) | collective-permute-done | bytes 32800 | tf_op jit(solution)/shard_map/ppermute | solution.py:34
  62.5 0.7 %copy-done.2 = f32[4,64,128]{2,1,0:T(8,128)} copy-done((f32[4,64,128]{2,1,0:T(8,128)}, f32[4,64,128]{2,1,0:T(8,128)S(1)}, u32[]{:S(2)}) %copy-start.2) | copy-done | bytes 131096
  (20 shorter events, 0.6 us)
Async XLA Ops:
  4.2 27.4 %all-to-all-start = ((bf16[32,2,16,128]{3,2,1,0:T(8,128)(2,1)}), bf16[32,2,16,128]{3,2,1,0:T(8,128)(2,1)S(1)}, u32[]{:S(2)}, u32[]{:S(2)}) async-start(bf16[32,2,16,128]{3,2,1,0:T(8,128)(2,1)} %get-tuple-element.30), calls=%async_computation | async-start | bytes 524288 | tf_op jit(solution)/shard_map/all_to_all | solution.py:291
  15.6 11.4 %collective-permute-start = (bf16[2,4,32,128]{3,2,1,0:T(8,128)(2,1)S(1)}, bf16[2,4,32,128]{3,2,1,0:T(8,128)(2,1)S(1)}, u32[]{:S(2)}, u32[]{:S(2)}) collective-permute-start(bf16[2,4,32,128]{3,2,1,0:T(8,128)(2,1)S(1)} %bitcast.17), channel_id=1, source_target_pairs={{240,248},{248,240},{0,8},{8,0},{244,252},{252,244},{4,12},{12,4},... | collective-permute-start | bytes 196616 | tf_op jit(solution)/shard_map/ppermute | solution.py:34
  15.9 11.1 %collective-permute-start.1 = (bf16[2,4,32,128]{3,2,1,0:T(8,128)(2,1)S(1)}, bf16[2,4,32,128]{3,2,1,0:T(8,128)(2,1)S(1)}, u32[]{:S(2)}, u32[]{:S(2)}) collective-permute-start(bf16[2,4,32,128]{3,2,1,0:T(8,128)(2,1)S(1)} %bitcast.18), channel_id=1, source_target_pairs={{240,0},{248,8},{0,240},{8,248},{244,4},{252,12},{4,244},{12,252},... | collective-permute-start | bytes 196616 | tf_op jit(solution)/shard_map/ppermute | solution.py:34
  22.0 9.5 %collective-permute-start.2 = (bf16[2,4,32,128]{3,2,1,0:T(8,128)(2,1)S(1)}, bf16[2,4,32,128]{3,2,1,0:T(8,128)(2,1)S(1)}, u32[]{:S(2)}, u32[]{:S(2)}) collective-permute-start(bf16[2,4,32,128]{3,2,1,0:T(8,128)(2,1)S(1)} %bitcast.19), channel_id=1, source_target_pairs={{240,8},{248,0},{0,248},{8,240},{244,12},{252,4},{4,252},{12,244},... | collective-permute-start | bytes 196616 | tf_op jit(solution)/shard_map/ppermute | solution.py:34
  23.4 30.5 %copy-start = (bf16[2048,128]{1,0:T(8,128)(2,1)S(1)}, bf16[2048,128]{1,0:T(8,128)(2,1)}, u32[]{:S(2)}) copy-start(bf16[2048,128]{1,0:T(8,128)(2,1)} %label_ref.1) | copy-start | bytes 1572868
  23.4 30.5 %copy-start.1 = (f32[2048]{0:T(1024)S(1)}, f32[2048]{0:T(1024)}, u32[]{:S(2)}) copy-start(f32[2048]{0:T(1024)} %param.10) | copy-start | bytes 24580
  31.5 1.6 %collective-permute-start.3 = (bf16[4,2,4,32,128]{4,3,2,1,0:T(8,128)(2,1)S(1)}, bf16[4,2,4,32,128]{4,3,2,1,0:T(8,128)(2,1)S(1)}, u32[]{:S(2)}, u32[]{:S(2)}) collective-permute-start(bf16[4,2,4,32,128]{4,3,2,1,0:T(8,128)(2,1)S(1)} %pad_maximum_fusion.refs_0_), channel_id=1, source_target_pairs={{0,4},{4,0},{8,12},{12,8},{16,20},{20,16},{24,28},{28,24},{32,36},... | collective-permute-start | bytes 786440 | tf_op jit(solution)/shard_map/ppermute | solution.py:312
  31.6 1.9 %collective-permute-start.4 = (bf16[32,2,16,128]{3,2,1,0:T(8,128)(2,1)S(1)}, bf16[32,2,16,128]{3,2,1,0:T(8,128)(2,1)S(1)}, u32[]{:S(2)}, u32[]{:S(2)}) collective-permute-start(bf16[32,2,16,128]{3,2,1,0:T(8,128)(2,1)S(1)} %all-to-all-done.refs_2_), channel_id=1, source_target_pairs={{0,4},{4,0},{8,12},{12,8},{16,20},{20,16},{24,28},{28,24},{32,36},... | collective-permute-start | bytes 786440 | tf_op jit(solution)/shard_map/ppermute | solution.py:313
  36.6 9.6 %collective-permute-start.7 = (bf16[128,1024]{1,0:T(8,128)(2,1)S(1)}, bf16[128,1024]{1,0:T(8,128)(2,1)S(1)}, u32[]{:S(2)}, u32[]{:S(2)}) collective-permute-start(bf16[128,1024]{1,0:T(8,128)(2,1)S(1)} %get-tuple-element.34), channel_id=1, source_target_pairs={{0,3},{1,2},{2,1},{3,0},{4,7},{5,6},{6,5},{7,4},{8,11},{9,10},{10,... | collective-permute-start | bytes 786440 | tf_op jit(solution)/shard_map/ppermute | solution.py:334
  39.5 8.1 %collective-permute-start.5 = (bf16[128,1024]{1,0:T(8,128)(2,1)S(1)}, bf16[128,1024]{1,0:T(8,128)(2,1)S(1)}, u32[]{:S(2)}, u32[]{:S(2)}) collective-permute-start(bf16[128,1024]{1,0:T(8,128)(2,1)S(1)} %get-tuple-element.32), channel_id=1, source_target_pairs={{0,1},{1,0},{2,3},{3,2},{4,5},{5,4},{6,7},{7,6},{8,9},{9,8},{10,11... | collective-permute-start | bytes 786440 | tf_op jit(solution)/shard_map/ppermute | solution.py:334
  46.3 5.1 %collective-permute-start.8 = (bf16[64,1024]{1,0:T(8,128)(2,1)S(1)}, bf16[64,1024]{1,0:T(8,128)(2,1)S(1)}, u32[]{:S(2)}, u32[]{:S(2)}) collective-permute-start(bf16[64,1024]{1,0:T(8,128)(2,1)S(1)} %add_convert_fusion), channel_id=1, source_target_pairs={{0,1},{1,0},{2,3},{3,2},{4,5},{5,4},{6,7},{7,6},{8,9},{9,8},{10,11... | collective-permute-start | bytes 393224 | tf_op jit(solution)/shard_map/ppermute | solution.py:334
  47.6 6.3 %collective-permute-start.6 = (bf16[64,1024]{1,0:T(8,128)(2,1)S(1)}, bf16[64,1024]{1,0:T(8,128)(2,1)S(1)}, u32[]{:S(2)}, u32[]{:S(2)}) collective-permute-start(bf16[64,1024]{1,0:T(8,128)(2,1)S(1)} %add_convert_fusion.1), channel_id=1, source_target_pairs={{0,3},{1,2},{2,1},{3,0},{4,7},{5,6},{6,5},{7,4},{8,11},{9,10},{10,... | collective-permute-start | bytes 393224 | tf_op jit(solution)/shard_map/ppermute | solution.py:334
  54.1 4.8 %collective-permute-start.9 = (f32[64,128]{1,0:T(8,128)S(1)}, f32[64,128]{1,0:T(8,128)S(1)}, u32[]{:S(2)}, u32[]{:S(2)}) collective-permute-start(f32[64,128]{1,0:T(8,128)S(1)} %logits.1), channel_id=1, source_target_pairs={{0,1},{1,0},{2,3},{3,2},{4,5},{5,4},{6,7},{7,6},{8,9},{9,8},{10,11... | collective-permute-start | bytes 98312 | tf_op jit(solution)/shard_map/ppermute | solution.py:34
  54.2 5.5 %collective-permute-start.10 = (f32[64,128]{1,0:T(8,128)S(1)}, f32[64,128]{1,0:T(8,128)S(1)}, u32[]{:S(2)}, u32[]{:S(2)}) collective-permute-start(f32[64,128]{1,0:T(8,128)S(1)} %logits.1), channel_id=1, source_target_pairs={{0,2},{1,3},{2,0},{3,1},{4,6},{5,7},{6,4},{7,5},{8,10},{9,11},{10,... | collective-permute-start | bytes 98312 | tf_op jit(solution)/shard_map/ppermute | solution.py:34
  57.3 5.1 %collective-permute-start.11 = (f32[64,128]{1,0:T(8,128)S(1)}, f32[64,128]{1,0:T(8,128)S(1)}, u32[]{:S(2)}, u32[]{:S(2)}) collective-permute-start(f32[64,128]{1,0:T(8,128)S(1)} %logits.1), channel_id=1, source_target_pairs={{0,3},{1,2},{2,1},{3,0},{4,7},{5,6},{6,5},{7,4},{8,11},{9,10},{10,... | collective-permute-start | bytes 98312 | tf_op jit(solution)/shard_map/ppermute | solution.py:34
  62.5 0.7 %copy-start.2 = (f32[4,64,128]{2,1,0:T(8,128)}, f32[4,64,128]{2,1,0:T(8,128)S(1)}, u32[]{:S(2)}) copy-start(f32[4,64,128]{2,1,0:T(8,128)S(1)} %bitcast_dynamic-update-slice_fusion) | copy-start | bytes 393220
